TPU v7x, 32 devices: a whole 2x2x4 slice. The times are simulated.
32 devices in a mesh: aa: 8 (over z, x), ba: 4 (over y, core).
Axes of the slice: x: 2, y: 2, z: 4, core: 2. Of those that a mesh axis runs over, the one named last changes fastest.
Arguments:
- features_a: bfloat16 [16, 32, 256], P('aa', 'ba'), may hold values from -9 to 9
- features_b: bfloat16 [16, 128, 256], P('ba', 'aa'), may hold values from -9 to 9
- conv_in: float32 [8, 3, 3, 3, 3], replicated, may hold values from -0.625 to 0.625
- bias_in: float32 [8], replicated, may hold values from -1 to 1
- conv_out: float32 [8, 3, 3, 3, 3], replicated, may hold values from -0.25 to 0.25
Outputs:
- log_mutual: float32 [16, 32, 16, 128], P('aa', None, 'ba')
- warped: float32 [16, 32, 256], P('aa', 'ba')
All inputs are finite; a program needn't handle non-finite values.
Results may differ from a plain program's by a relative error of at most 0.0035.
Values may be sent and summed in bfloat16 or wider, within the bound.
No kernel may reach another device: no remote copies, remote signals or barrier semaphores. Data moves between devices by JAX's collectives and lax.ppermute only.
A program may use at most 64 MiB of HBM per device.

v0:
```python
import math

import jax
import jax.numpy as jnp
from jax import lax
from jax.sharding import PartitionSpec as P


def padded_2(cells, sides, width):
    for axis, dim in sides:
        count = lax.axis_size(axis)
        ends = count - 1
        head = lax.slice_in_dim(cells, 0, width, axis=dim)
        tail = lax.slice_in_dim(cells, cells.shape[dim] - width, cells.shape[dim], axis=dim)
        cells = jnp.concatenate(
            [
                lax.ppermute(tail, axis, [(i, (i + 1) % count) for i in range(ends)]),
                cells,
                lax.ppermute(head, axis, [((i + 1) % count, i) for i in range(ends)]),
            ],
            axis=dim,
        )
    return cells


def tap_offsets():
    return [
        (step_one, step_two, step_three, step_four)
        for step_one in range(3)
        for step_two in range(3)
        for step_three in range(3)
        for step_four in range(3)
    ]


def spread_taps(padded, kernel, bias_in):
    extent = [size_here - 2 for size_here in padded.shape]
    result = jnp.zeros([kernel.shape[0]] + extent, jnp.float32)
    for offsets in tap_offsets():
        window = padded[
            offsets[0] : offsets[0] + extent[0],
            offsets[1] : offsets[1] + extent[1],
            offsets[2] : offsets[2] + extent[2],
            offsets[3] : offsets[3] + extent[3],
        ]
        result = (
            result
            + kernel[:, offsets[0], offsets[1], offsets[2], offsets[3]].reshape(-1, 1, 1, 1, 1)
            * window[None]
        )
    return jax.nn.relu(result + bias_in.reshape(-1, 1, 1, 1, 1))


def reduce_taps(padded, kernel):
    extent = [size_here - 2 for size_here in padded.shape[1:]]
    result = jnp.zeros(extent, jnp.float32)
    for offsets in tap_offsets():
        window = padded[
            :,
            offsets[0] : offsets[0] + extent[0],
            offsets[1] : offsets[1] + extent[1],
            offsets[2] : offsets[2] + extent[2],
            offsets[3] : offsets[3] + extent[3],
        ]
        result = result + jnp.sum(
            kernel[:, offsets[0], offsets[1], offsets[2], offsets[3]].reshape(-1, 1, 1, 1, 1)
            * window,
            axis=0,
        )
    return result


def dual_norms(values):
    top_a = lax.pmax(jnp.max(values, axis=(0, 1)), "aa")
    top_b = lax.pmax(jnp.max(values, axis=(2, 3)), "ba")
    mass_a = lax.psum(jnp.sum(jnp.exp(values - top_a), axis=(0, 1)), "aa")
    mass_b = lax.psum(jnp.sum(jnp.exp(values - top_b[:, :, None, None]), axis=(2, 3)), "ba")
    norm_a = top_a + jnp.log(mass_a)
    norm_b = top_b + jnp.log(mass_b)
    return (norm_a, norm_b[:, :, None, None])


def local(features_a, features_b, conv_in, bias_in, conv_out):
    channels = features_a.shape[2]
    rows_a = lax.all_gather(features_a, "ba", axis=1, tiled=True)
    rows_b = lax.all_gather(features_b, "aa", axis=1, tiled=True)
    height_a = rows_a.shape[0]
    width_a = rows_a.shape[1]
    height_b = rows_b.shape[0]
    width_b = rows_b.shape[1]
    grid_a = height_a * lax.axis_size("aa")
    grid_b = height_b * lax.axis_size("ba")
    offset = math.log(grid_a * width_a * grid_b * width_b)
    scores = jnp.einsum(
        "xyc,uvc->xyuv", rows_a, rows_b, preferred_element_type=jnp.float32
    ) / math.sqrt(channels)
    norm_a, norm_b = dual_norms(scores)
    matched = jax.nn.softplus(2.0 * scores - norm_a - norm_b + offset)
    rim = padded_2(matched, (("aa", 0), ("ba", 2)), 1)
    hidden = spread_taps(jnp.pad(rim, ((0, 0), (1, 1), (0, 0), (1, 1))), conv_in, bias_in)
    rim_hidden = padded_2(hidden, (("aa", 1), ("ba", 3)), 1)
    filtered = reduce_taps(jnp.pad(rim_hidden, ((0, 0), (0, 0), (1, 1), (0, 0), (1, 1))), conv_out)
    refined = scores + jax.nn.relu(filtered)
    norm_a2, norm_b2 = dual_norms(refined)
    log_mutual = 2.0 * refined - norm_a2 - norm_b2 + offset
    weights = jnp.exp(refined - norm_b2).astype(jnp.bfloat16)
    transfer_terms = jnp.einsum(
        "xyuv,uvc->xyc", weights, rows_b, preferred_element_type=jnp.float32
    )
    warped = lax.psum_scatter(transfer_terms, "ba", scatter_dimension=1, tiled=True)
    return (log_mutual, warped)


def solution(mesh):
    placed = (P("aa", "ba", None), P("ba", "aa", None), P(), P(), P())
    return jax.shard_map(
        local,
        mesh=mesh,
        in_specs=placed,
        out_specs=(P("aa", None, "ba", None), P("aa", "ba", None)),
        check_vma=False,
    )
```

profile of v0, /device:TPU:0, one launch (start us, length us, event | category | flops | bytes accessed | tf_op | source)
XLA Modules:
  0.0 315.7 jit_solution(11921888077074273181)
XLA Ops:
  7.2 32.8 %all_gather.7 = bf16[4,128,256]{2,1,0:T(8,128)(2,1)S(1)} all-gather(bf16[4,16,256]{2,1,0:T(8,128)(2,1)} %param.6), channel_id=1, replica_groups=mesh['aa'=8,'ba'=4] {'aa'}, dimensions={1}, use_global_device_ids=true | all-gather | bytes 294912 | tf_op jit(solution)/shard_map/all_gather | solution.py:86
  40.0 5.4 %all_gather.6 = bf16[2,32,256]{2,1,0:T(8,128)(2,1)S(1)} all-gather(bf16[2,8,256]{2,1,0:T(8,128)(2,1)} %param.5), channel_id=1, replica_groups=mesh['aa'=8,'ba'=4] {'ba'}, dimensions={1}, use_global_device_ids=true | all-gather | bytes 40960 | tf_op jit(solution)/shard_map/all_gather | solution.py:85
  45.6 21.4 %pmax.28 = f32[4,128]{1,0:T(4,128)S(1)} all-reduce(f32[4,128]{1,0:T(4,128)S(1)} %get-tuple-element.348), channel_id=1, replica_groups=mesh['aa'=8,'ba'=4] {'aa'}, use_global_device_ids=true, to_apply=%region_1.0 | all-reduce | flops 512 | bytes 4096 | tf_op jit(solution)/shard_map/pmax | solution.py:74
  67.1 5.7 %pmax.29 = f32[2,32]{1,0:T(2,128)S(1)} all-reduce(f32[2,32]{1,0:T(2,128)S(1)} %get-tuple-element.92), channel_id=1, replica_groups=mesh['aa'=8,'ba'=4] {'ba'}, use_global_device_ids=true, to_apply=%region_5.0 | all-reduce | flops 64 | bytes 512 | tf_op jit(solution)/shard_map/pmax | solution.py:75
  72.9 6.6 %psum.29 = f32[2,32]{1,0:T(2,128)S(1)} all-reduce(f32[2,32]{1,0:T(2,128)S(1)} %exponential_reduce_fusion.2), channel_id=1, replica_groups=mesh['aa'=8,'ba'=4] {'ba'}, use_global_device_ids=true, to_apply=%region_7.0 | all-reduce | flops 64 | bytes 512 | tf_op jit(solution)/shard_map/psum | solution.py:77
  79.6 17.1 %psum.28 = f32[4,128]{1,0:T(4,128)S(1)} all-reduce(f32[4,128]{1,0:T(4,128)S(1)} %get-tuple-element.91), channel_id=1, replica_groups=mesh['aa'=8,'ba'=4] {'aa'}, use_global_device_ids=true, to_apply=%region_3.0 | all-reduce | flops 512 | bytes 4096 | tf_op jit(solution)/shard_map/psum | solution.py:76
  96.9 4.0 %collective-permute-start = (f32[1,32,4,128]{3,1,2,0:T(8,128)S(1)}, f32[1,32,4,128]{3,1,2,0:T(8,128)S(1)}, u32[]{:S(2)}, u32[]{:S(2)}) collective-permute-start(f32[1,32,4,128]{3,1,2,0:T(8,128)S(1)} %get-tuple-element.184), channel_id=1, source_target_pairs={{0,4},{4,8},{8,12},{12,16},{16,20},{20,24},{24,28},{1,5},{5,9},{9,... | collective-permute-start | bytes 196616 | tf_op jit(solution)/shard_map/ppermute | solution.py:17
  100.8 1.3 collective-permute-start.1
  102.1 1.5 slice_bitcast_fusion.160
  103.6 1.5 slice_bitcast_fusion.159
  105.2 1.5 slice_bitcast_fusion.158
  106.7 1.5 slice_bitcast_fusion.157
  108.2 1.3 slice_bitcast_fusion.156
  109.6 1.3 collective-permute-start.2
  110.9 1.6 collective-permute-start.3
  112.8 2.4 collective-permute-done.3
  121.8 0.8 copy.120
  147.6 0.7 copy.161
  153.5 0.8 copy.89
  166.7 12.5 %add_maximum_fusion = f32[8,2,32,4,128]{4,0,3,2,1:T(8,128)S(1)} fusion(f32[8]{0:T(128)} %param.8, f32[2,32,4,128]{3,2,1,0:T(4,128)} %copy.169, f32[8]{0:T(128)} %get-tuple-element.346, f32[2,32,4,128]{3,2,1,0:T(4,128)} %copy.168, f32[8]{0:T(128)} %get-tuple-element.347, f32[2,32,4,128]{3,2,1,0:T(4,128)} %copy.167, f32[8]{0:T(128)S(1)} %get-tuple-element.268, ...), kind=kLoop, calls=%fused_computation.181 | loop fusion | flops 42729472 | bytes 11668032 | tf_op jit(solution)/shard_map/jit(relu)/max | solution.py:51
  179.3 4.6 %collective-permute-start.4 = (f32[8,1,32,4,128]{4,0,3,2,1:T(8,128)S(1)}, f32[8,1,32,4,128]{4,0,3,2,1:T(8,128)S(1)}, u32[]{:S(2)}, u32[]{:S(2)}) collective-permute-start(f32[8,1,32,4,128]{4,0,3,2,1:T(8,128)S(1)} %get-tuple-element.98), channel_id=1, source_target_pairs={{0,4},{4,8},{8,12},{12,16},{16,20},{20,24},{24,28},{1,5},{5,9},{9,... | collective-permute-start | bytes 1572872 | tf_op jit(solution)/shard_map/ppermute | solution.py:17
  183.8 1.3 collective-permute-start.5
  185.1 0.9 slice_bitcast_fusion.62
  186.0 0.9 slice_bitcast_fusion.60
  186.9 0.9 slice_bitcast_fusion.59
  187.8 17.6 %collective-permute-done.4 = f32[8,1,32,4,128]{4,0,3,2,1:T(8,128)S(1)} collective-permute-done((f32[8,1,32,4,128]{4,0,3,2,1:T(8,128)S(1)}, f32[8,1,32,4,128]{4,0,3,2,1:T(8,128)S(1)}, u32[]{:S(2)}, u32[]{:S(2)}) %collective-permute-start.4) | collective-permute-done | bytes 524320 | tf_op jit(solution)/shard_map/ppermute | solution.py:17
  205.5 4.0 %collective-permute-start.6 = (f32[8,4,32,1,128]{4,0,3,2,1:T(8,128)S(1)}, f32[8,4,32,1,128]{4,0,3,2,1:T(8,128)S(1)}, u32[]{:S(2)}, u32[]{:S(2)}) collective-permute-start(f32[8,4,32,1,128]{4,0,3,2,1:T(8,128)S(1)} %get-tuple-element.96), channel_id=1, source_target_pairs={{0,1},{1,2},{2,3},{4,5},{5,6},{6,7},{8,9},{9,10},{10,11},{12,13},{... | collective-permute-start | bytes 1572872 | tf_op jit(solution)/shard_map/ppermute | solution.py:17
  209.5 1.3 collective-permute-start.7
  210.8 1.4 slice_bitcast_fusion.78
  212.2 1.5 slice_bitcast_fusion.61
  213.7 1.7 fusion.71
  215.8 1.7 fusion.74
  217.5 1.7 fusion.67
  219.2 3.9 %select_maximum_fusion = f32[8,4,34,6,130]{4,0,3,2,1:T(8,128)S(1)} fusion(f32[8,4,32,1,128]{4,0,3,2,1:T(8,128)S(1)} %collective-permute-done.7, f32[8,4,32,1,128]{4,0,3,2,1:T(8,128)S(1)} %collective-permute-done.6, f32[8,1,32,4,128]{4,0,3,2,1:T(8,128)S(1)} %collective-permute-done.5, f32[8,2,32,4,128]{4,0,3,2,1:T(8,128)S(1)} %add_maximum_fusion, ...), kind=kLoop, calls=%fused_computation.4 | loop fusion | flops 17821440 | bytes 6540288 | tf_op jit(solution)/shard_map/concatenate | solution.py:15
  223.1 3.2 fusion.81
  226.3 3.2 %fusion.80 = (f32[2,32,4,128]{3,2,1,0:T(4,128)S(1)}, f32[2,32,4,128]{3,2,1,0:T(4,128)S(1)}, f32[2,32,4,128]{3,2,1,0:T(4,128)S(1)}, f32[2,32,4,128]{3,2,1,0:T(4,1...) fusion(f32[8,4,34,6,130]{4,0,3,2,1:T(8,128)S(1)} %select_maximu, ...), kind=kLoop, calls=%fused_computation.171 | loop fusion | flops 4423680 | bytes 10617120 | tf_op jit(solution)/shard_map/reduce_sum | solution.py:65
  229.5 3.3 %fusion.79 = (f32[2,32,4,128]{3,2,1,0:T(4,128)S(1)}, f32[2,32,4,128]{3,2,1,0:T(4,128)S(1)}, f32[2,32,4,128]{3,2,1,0:T(4,128)S(1)}, f32[2,32,4,128]{3,2,1,0:T(4,1...) fusion(f32[8,4,34,6,130]{4,0,3,2,1:T(8,128)S(1)} %select_maximu, ...), kind=kLoop, calls=%fused_computation.169 | loop fusion | flops 4423680 | bytes 10617120 | tf_op jit(solution)/shard_map/reduce_sum | solution.py:65
  232.8 3.4 %fusion.78 = (f32[2,32,4,128]{3,2,1,0:T(4,128)S(1)}, f32[2,32,4,128]{3,2,1,0:T(4,128)S(1)}, f32[2,32,4,128]{3,2,1,0:T(4,128)S(1)}, f32[2,32,4,128]{3,2,1,0:T(4,1...) fusion(f32[8,4,34,6,130]{4,0,3,2,1:T(8,128)S(1)} %select_maximu, ...), kind=kLoop, calls=%fused_computation.167 | loop fusion | flops 4423680 | bytes 10617120 | tf_op jit(solution)/shard_map/reduce_sum | solution.py:65
  236.3 3.2 %fusion.83 = (f32[2,32,4,128]{3,2,1,0:T(4,128)S(1)}, f32[2,32,4,128]{3,2,1,0:T(4,128)S(1)}, f32[2,32,4,128]{3,2,1,0:T(4,128)S(1)}, f32[2,32,4,128]{3,2,1,0:T(4,1...) fusion(f32[8,4,34,6,130]{4,0,3,2,1:T(8,128)S(1)} %select_maximu, ...), kind=kLoop, calls=%fused_computation.177 | loop fusion | flops 4423680 | bytes 10617120 | tf_op jit(solution)/shard_map/reduce_sum | solution.py:65
  239.6 4.1 %fusion.82 = (f32[2,32,4,128]{3,2,1,0:T(4,128)}, f32[2,32,4,128]{3,2,1,0:T(4,128)}, f32[2,32,4,128]{3,2,1,0:T(4,128)}, f32[2,32,4,128]{3,2,1,0:T(4,128)}, f32[2,...) fusion(f32[8,4,34,6,130]{4,0,3,2,1:T(8,128)S(1)} %select_maximu, ...), kind=kLoop, calls=%fused_computation.175 | loop fusion | flops 4423680 | bytes 10617120 | tf_op jit(solution)/shard_map/reduce_sum | solution.py:65
  243.8 4.1 %fusion.84 = (f32[2,32,4,128]{3,2,1,0:T(4,128)}, f32[2,32,4,128]{3,2,1,0:T(4,128)}, f32[2,32,4,128]{3,2,1,0:T(4,128)}, f32[2,32,4,128]{3,2,1,0:T(4,128)}, f32[2,...) fusion(f32[8,4,34,6,130]{4,0,3,2,1:T(8,128)S(1)} %select_maximu, ...), kind=kLoop, calls=%fused_computation.179 | loop fusion | flops 4423680 | bytes 10617120 | tf_op jit(solution)/shard_map/reduce_sum | solution.py:65
  247.8 4.3 %fusion.77 = (f32[2,32,4,128]{3,2,1,0:T(4,128)}, f32[2,32,4,128]{3,2,1,0:T(4,128)}, f32[2,32,4,128]{3,2,1,0:T(4,128)}, f32[2,32,4,128]{3,2,1,0:T(4,128)}, f32[2,...) fusion(f32[8,4,34,6,130]{4,0,3,2,1:T(8,128)S(1)} %select_maximu, ...), kind=kLoop, calls=%fused_computation.165 | loop fusion | flops 4423680 | bytes 10617120 | tf_op jit(solution)/shard_map/reduce_sum | solution.py:65
  252.1 3.1 fusion.95
  255.2 19.3 %pmax.30 = f32[4,128]{1,0:T(4,128)S(1)} all-reduce(f32[4,128]{1,0:T(4,128)S(1)} %get-tuple-element.89), channel_id=1, replica_groups=mesh['aa'=8,'ba'=4] {'aa'}, use_global_device_ids=true, to_apply=%region_90.91 | all-reduce | flops 512 | bytes 4096 | tf_op jit(solution)/shard_map/pmax | solution.py:74
  274.5 7.8 %pmax.31 = f32[2,32]{1,0:T(2,128)S(1)} all-reduce(f32[2,32]{1,0:T(2,128)S(1)} %get-tuple-element.90), channel_id=1, replica_groups=mesh['aa'=8,'ba'=4] {'ba'}, use_global_device_ids=true, to_apply=%region_94.95 | all-reduce | flops 64 | bytes 512 | tf_op jit(solution)/shard_map/pmax | solution.py:75
  282.5 7.2 %psum.31 = f32[2,32]{1,0:T(2,128)S(1)} all-reduce(f32[2,32]{1,0:T(2,128)S(1)} %get-tuple-element.88), channel_id=1, replica_groups=mesh['aa'=8,'ba'=4] {'ba'}, use_global_device_ids=true, to_apply=%region_96.97 | all-reduce | flops 64 | bytes 512 | tf_op jit(solution)/shard_map/psum | solution.py:77
  289.8 0.8 convolution_bitcast_fusion
  290.6 17.1 %psum.30 = f32[4,128]{1,0:T(4,128)S(1)} all-reduce(f32[4,128]{1,0:T(4,128)S(1)} %get-tuple-element.87), channel_id=1, replica_groups=mesh['aa'=8,'ba'=4] {'aa'}, use_global_device_ids=true, to_apply=%region_92.93 | all-reduce | flops 512 | bytes 4096 | tf_op jit(solution)/shard_map/psum | solution.py:76
  (135 shorter events, 51.8 us)
Async XLA Ops:
  7.2 301.4 %reduce-scatter.2.cloned.1.call-start = ((), (), s32[]{:S(2)}) async-start(), calls=%async_computation.1 | async-start | bytes 81920 | tf_op jit(solution)/shard_map/reduce_scatter | solution.py:110
  96.9 12.7 %collective-permute-start = (f32[1,32,4,128]{3,1,2,0:T(8,128)S(1)}, f32[1,32,4,128]{3,1,2,0:T(8,128)S(1)}, u32[]{:S(2)}, u32[]{:S(2)}) collective-permute-start(f32[1,32,4,128]{3,1,2,0:T(8,128)S(1)} %get-tuple-element.184), channel_id=1, source_target_pairs={{0,4},{4,8},{8,12},{12,16},{16,20},{20,24},{24,28},{1,5},{5,9},{9,... | collective-permute-start | bytes 196616 | tf_op jit(solution)/shard_map/ppermute | solution.py:17
  100.8 8.8 %collective-permute-start.1 = (f32[1,32,4,128]{3,1,2,0:T(8,128)S(1)}, f32[1,32,4,128]{3,1,2,0:T(8,128)S(1)}, u32[]{:S(2)}, u32[]{:S(2)}) collective-permute-start(f32[1,32,4,128]{3,1,2,0:T(8,128)S(1)} %get-tuple-element.185), channel_id=1, source_target_pairs={{4,0},{8,4},{12,8},{16,12},{20,16},{24,20},{28,24},{5,1},{9,5},{13... | collective-permute-start | bytes 196616 | tf_op jit(solution)/shard_map/ppermute | solution.py:19
  109.6 3.1 collective-permute-start.2
  110.9 4.2 %collective-permute-start.3 = (f32[4,32,1,128]{3,1,2,0:T(8,128)S(1)}, f32[4,32,1,128]{3,1,2,0:T(8,128)S(1)}, u32[]{:S(2)}, u32[]{:S(2)}) collective-permute-start(f32[4,32,1,128]{3,1,2,0:T(8,128)S(1)} %get-tuple-element.181), channel_id=1, source_target_pairs={{1,0},{2,1},{3,2},{5,4},{6,5},{7,6},{9,8},{10,9},{11,10},{13,12},{... | collective-permute-start | bytes 196616 | tf_op jit(solution)/shard_map/ppermute | solution.py:19
  179.3 26.1 %collective-permute-start.4 = (f32[8,1,32,4,128]{4,0,3,2,1:T(8,128)S(1)}, f32[8,1,32,4,128]{4,0,3,2,1:T(8,128)S(1)}, u32[]{:S(2)}, u32[]{:S(2)}) collective-permute-start(f32[8,1,32,4,128]{4,0,3,2,1:T(8,128)S(1)} %get-tuple-element.98), channel_id=1, source_target_pairs={{0,4},{4,8},{8,12},{12,16},{16,20},{20,24},{24,28},{1,5},{5,9},{9,... | collective-permute-start | bytes 1572872 | tf_op jit(solution)/shard_map/ppermute | solution.py:17
  183.8 21.5 %collective-permute-start.5 = (f32[8,1,32,4,128]{4,0,3,2,1:T(8,128)S(1)}, f32[8,1,32,4,128]{4,0,3,2,1:T(8,128)S(1)}, u32[]{:S(2)}, u32[]{:S(2)}) collective-permute-start(f32[8,1,32,4,128]{4,0,3,2,1:T(8,128)S(1)} %get-tuple-element.99), channel_id=1, source_target_pairs={{4,0},{8,4},{12,8},{16,12},{20,16},{24,20},{28,24},{5,1},{9,5},{13... | collective-permute-start | bytes 1572872 | tf_op jit(solution)/shard_map/ppermute | solution.py:19
  205.5 9.9 %collective-permute-start.6 = (f32[8,4,32,1,128]{4,0,3,2,1:T(8,128)S(1)}, f32[8,4,32,1,128]{4,0,3,2,1:T(8,128)S(1)}, u32[]{:S(2)}, u32[]{:S(2)}) collective-permute-start(f32[8,4,32,1,128]{4,0,3,2,1:T(8,128)S(1)} %get-tuple-element.96), channel_id=1, source_target_pairs={{0,1},{1,2},{2,3},{4,5},{5,6},{6,7},{8,9},{9,10},{10,11},{12,13},{... | collective-permute-start | bytes 1572872 | tf_op jit(solution)/shard_map/ppermute | solution.py:17
  209.5 5.9 %collective-permute-start.7 = (f32[8,4,32,1,128]{4,0,3,2,1:T(8,128)S(1)}, f32[8,4,32,1,128]{4,0,3,2,1:T(8,128)S(1)}, u32[]{:S(2)}, u32[]{:S(2)}) collective-permute-start(f32[8,4,32,1,128]{4,0,3,2,1:T(8,128)S(1)} %get-tuple-element.97), channel_id=1, source_target_pairs={{1,0},{2,1},{3,2},{5,4},{6,5},{7,6},{9,8},{10,9},{11,10},{13,12},{... | collective-permute-start | bytes 1572872 | tf_op jit(solution)/shard_map/ppermute | solution.py:19
  232.8 3.5 %copy-start.3 = (f32[8]{0:T(128)S(1)}, f32[8]{0:T(128)}, u32[]{:S(2)}) copy-start(f32[8]{0:T(128)} %get-tuple-element.263) | copy-start | bytes 100
  236.2 3.4 %copy-start.2 = (f32[8]{0:T(128)S(1)}, f32[8]{0:T(128)}, u32[]{:S(2)}) copy-start(f32[8]{0:T(128)} %get-tuple-element.262) | copy-start | bytes 100
  236.2 3.4 %copy-start.4 = (f32[8]{0:T(128)S(1)}, f32[8]{0:T(128)}, u32[]{:S(2)}) copy-start(f32[8]{0:T(128)} %get-tuple-element.206) | copy-start | bytes 100
  236.2 3.4 %copy-start.5 = (f32[8]{0:T(128)S(1)}, f32[8]{0:T(128)}, u32[]{:S(2)}) copy-start(f32[8]{0:T(128)} %get-tuple-element.207) | copy-start | bytes 100
  236.2 3.4 %copy-start.6 = (f32[8]{0:T(128)S(1)}, f32[8]{0:T(128)}, u32[]{:S(2)}) copy-start(f32[8]{0:T(128)} %get-tuple-element.208) | copy-start | bytes 100
  236.2 3.4 %copy-start.7 = (f32[8]{0:T(128)S(1)}, f32[8]{0:T(128)}, u32[]{:S(2)}) copy-start(f32[8]{0:T(128)} %get-tuple-element.209) | copy-start | bytes 100
  236.2 3.4 %copy-start.8 = (f32[8]{0:T(128)S(1)}, f32[8]{0:T(128)}, u32[]{:S(2)}) copy-start(f32[8]{0:T(128)} %get-tuple-element.210) | copy-start | bytes 100
  236.2 3.4 %copy-start.9 = (f32[8]{0:T(128)S(1)}, f32[8]{0:T(128)}, u32[]{:S(2)}) copy-start(f32[8]{0:T(128)} %get-tuple-element.211) | copy-start | bytes 100
  236.3 3.4 %copy-start.10 = (f32[8]{0:T(128)S(1)}, f32[8]{0:T(128)}, u32[]{:S(2)}) copy-start(f32[8]{0:T(128)} %get-tuple-element.212) | copy-start | bytes 100
  236.3 3.4 %copy-start.11 = (f32[8]{0:T(128)S(1)}, f32[8]{0:T(128)}, u32[]{:S(2)}) copy-start(f32[8]{0:T(128)} %get-tuple-element.213) | copy-start | bytes 100
  239.5 4.2 %copy-start = (f32[8]{0:T(128)S(1)}, f32[8]{0:T(128)}, u32[]{:S(2)}) copy-start(f32[8]{0:T(128)} %get-tuple-element.264) | copy-start | bytes 100
  239.5 4.2 %copy-start.1 = (f32[8]{0:T(128)S(1)}, f32[8]{0:T(128)}, u32[]{:S(2)}) copy-start(f32[8]{0:T(128)} %get-tuple-element.266) | copy-start | bytes 100
Sparse Core Ops, SparseCore 0:
  290.7 16.0 reduce-scatter.1
where the time goes:
time: 319 us; the launch traced here: 316 us
  blocking collectives  140 us (44%)
  local copies, waits for them, and re-layouts  65 us (20%)
  other arithmetic  55 us (17%)
  waiting for transfers between devices  20 us (6%)
  starting transfers between devices  19.3 us (6%)
  between operations  14.9 us (5%)
    slice x85, local copies, waits for them, and re-layouts, spread_taps(): padded[offsets[0]:offsets[0] + extent[0], offsets[1]:offsets[1] + extent[...  51.2 us
    pmax x2, blocking collectives, dual_norms(): top_a = lax.pmax(jnp.max(values, axis=(0, 1)), 'aa')  40.7 us
    psum x2, blocking collectives, dual_norms(): mass_a = lax.psum(jnp.sum(jnp.exp(values - top_a), axis=(0, 1)), 'aa')  34.3 us
    reduce_sum x11, other arithmetic, reduce_taps(): jnp.sum(kernel[:, offsets[0], offsets[1], offsets[2], offsets[3]].reshape...  33.8 us
    all_gather x1, blocking collectives, local(): rows_b = lax.all_gather(features_b, 'aa', axis=1, tiled=True)  32.8 us
    ppermute x4, waiting for transfers between devices, padded_2(): lax.ppermute(tail, axis, [(i, (i + 1) % count) for i in range(ends)])  17.6 us
    psum x2, blocking collectives, dual_norms(): lax.psum(jnp.sum(jnp.exp(values - top_b[:, :, None, None]), axis=(2, 3)),...  13.9 us
    ppermute x4, starting transfers between devices, padded_2(): lax.ppermute(tail, axis, [(i, (i + 1) % count) for i in range(ends)])  13.8 us
  transfers between devices with their start and end apart: 9, of which 2 were waited for; matrix products, arithmetic and copies ran while one was open for 5% of the time, Pallas kernels for 0%

commit v1 on v0

v1 whole, which is shorter than its diff:
```python
import functools
import math

import jax
import jax.numpy as jnp
from jax import lax
from jax.experimental import pallas as pl
from jax.experimental.pallas import tpu as pltpu
from jax.sharding import PartitionSpec as P

F32 = jnp.float32
BF16 = jnp.bfloat16
NT = (((1,), (1,)), ((), ()))
NN = (((1,), (0,)), ((), ()))
BLOCK = 8
HALF = 64
LANES = 128


class Sizes:
    def __init__(self, rows_a, width_a, rows_b, width_b, channels, hidden, grid_a, grid_b):
        self.rows_a, self.width_a = rows_a, width_a
        self.rows_b, self.width_b = rows_b, width_b
        self.channels, self.hidden = channels, hidden
        self.grid_a, self.grid_b = grid_a, grid_b
        self.blocks = width_a // BLOCK
        self.halo_a = rows_a + 4
        self.halo_b = rows_b + 4
        self.mid_a = rows_a + 2
        self.mid_b = rows_b + 2
        self.span = BLOCK + 2
        self.lanes_in = self.blocks * HALF
        self.lanes_mid = hidden * self.mid_a * BLOCK
        self.cells_a = rows_a * width_a
        self.cells_b = rows_b * width_b
        self.offset = math.log(grid_a * width_a * grid_b * width_b)
        self.scale = 1.0 / math.sqrt(channels)
        assert self.halo_a * self.span <= HALF and self.cells_a == HALF
        assert width_b == LANES and self.lanes_mid % LANES == 0
        assert self.blocks % 2 == 0


def iota(shape, dim):
    return lax.broadcasted_iota(jnp.int32, shape, dim)


def over_span(index, span):
    return (index * (2048 // span + 1)) >> 11


def dot(left, right, dims=NN):
    return lax.dot_general(left, right, dims, preferred_element_type=F32)


def vmem_specs(count):
    return [pl.BlockSpec(memory_space=pltpu.VMEM)] * count


def smem_spec():
    return pl.BlockSpec(memory_space=pltpu.SMEM)


def patch_lanes(sz, shape, dim):
    index = iota(shape, dim)
    block = index >> 6
    inner = index & (HALF - 1)
    row = over_span(inner, sz.span)
    col = block * BLOCK + inner - row * sz.span - 1
    inside = (inner < sz.halo_a * sz.span) & (col >= 0) & (col < sz.width_a)
    return row, col, inside


def taps_kernel(sz, w_in_ref, w_out_ref, bias_ref, t_in_ref, t_out_ref, bias_row_ref, rows_ref, wide_ref):
    lanes = sz.lanes_mid
    per = sz.mid_a * BLOCK
    head = iota((sz.hidden, lanes), 0)
    lane = iota((sz.hidden, lanes), 1)
    pick = (lane >= head * per) & (lane < head * per + per)
    pick16 = pick.astype(F32).astype(BF16)
    rows_ref[...] = dot(w_in_ref[...].astype(BF16), pick16)
    bias_row_ref[...] = jnp.sum(jnp.where(pick, bias_ref[...], 0.0), axis=0, keepdims=True)
    inner = iota((HALF, lanes), 0)
    row_in = over_span(inner, sz.span)
    col_in = inner - row_in * sz.span
    lane = iota((HALF, lanes), 1)
    row_out = (lane // BLOCK) % sz.mid_a
    col_out = lane % BLOCK
    step_row = row_in - row_out
    step_col = col_in - col_out
    usable = inner < sz.halo_a * sz.span
    zeros = jnp.zeros((HALF, lanes), F32)
    for three in range(3):
        for four in range(3):
            total = zeros
            for one in range(3):
                for two in range(3):
                    tap = ((one * 3 + two) * 3 + three) * 3 + four
                    match = usable & (step_row == one) & (step_col == two)
                    total = jnp.where(match, rows_ref[tap : tap + 1, :], total)
            start = three * 4 * HALF + four * HALF
            t_in_ref[start : start + HALF, :] = total.astype(BF16)
        start = three * 4 * HALF + 3 * HALF
        t_in_ref[start : start + HALF, :] = zeros.astype(BF16)

    out_lanes = 4 * HALF
    unit = sz.rows_a * BLOCK
    group = 9 * sz.hidden
    for row in range(sz.mid_a):
        pair = iota((16, out_lanes), 0)
        lane = iota((16, out_lanes), 1)
        one = pair // 3
        four = pair - one * 3
        row_out = (lane % unit) // BLOCK
        hit = (pair < 9) & ((lane >> 6) == four) & (row - row_out == one)
        wide_ref[row * group : (row + 1) * group, :] = dot(
            w_out_ref[...].astype(BF16), hit.astype(F32).astype(BF16)
        )
    lane = iota((BLOCK, out_lanes), 1)
    col_out = ((lane & (HALF - 1)) // unit) * BLOCK + lane % BLOCK
    for block in range(sz.blocks):
        step = iota((BLOCK, out_lanes), 0) + block * BLOCK - col_out + 1
        for three in range(3):
            for head in range(sz.hidden):
                for row in range(0, sz.mid_a, 2):
                    parts = []
                    for sub in (row, row + 1):
                        total = jnp.zeros((BLOCK, out_lanes), F32)
                        for two in range(3):
                            at = sub * group + (two * 3 + three) * sz.hidden + head
                            total = jnp.where(step == two, wide_ref[at : at + 1, :], total)
                        parts.append(total)
                    start = three * sz.blocks * lanes + block * lanes + head * per + row * BLOCK
                    t_out_ref[start : start + 2 * BLOCK, :] = jnp.concatenate(parts, 0).astype(BF16)


def build_taps(sz, conv_in, bias_in, conv_out):
    hidden = conv_in.shape[0]
    w_in = jnp.transpose(conv_in, (1, 2, 3, 4, 0)).reshape(81, hidden)
    w_out = jnp.transpose(conv_out, (2, 3, 0, 1, 4)).reshape(9 * hidden, 9)
    w_out = jnp.pad(w_out, ((0, 0), (0, 7)))
    rows_in = 3 * 4 * HALF
    rows_out = 3 * sz.blocks * sz.lanes_mid
    return pl.pallas_call(
        functools.partial(taps_kernel, sz),
        out_shape=(
            jax.ShapeDtypeStruct((rows_in, sz.lanes_mid), BF16),
            jax.ShapeDtypeStruct((rows_out, 4 * HALF), BF16),
            jax.ShapeDtypeStruct((1, sz.lanes_mid), F32),
        ),
        in_specs=vmem_specs(3),
        out_specs=tuple(vmem_specs(3)),
        scratch_shapes=[
            pltpu.VMEM((81, sz.lanes_mid), F32),
            pltpu.VMEM((sz.mid_a * 9 * hidden, 4 * HALF), F32),
        ],
        name="taps",
    )(w_in, w_out, bias_in.reshape(hidden, 1))


def scores_body(sz, rank_ref, norm_rows, patch_rows, tile_b, u_ref, part_ref, own_ref):
    channels = sz.channels
    source = patch_rows.shape[0]
    row, col, inside = patch_lanes(sz, (sz.lanes_in, source), 0)
    at = iota((sz.lanes_in, source), 1)
    wanted = (col >> 3) * (sz.halo_a * BLOCK) + row * BLOCK + (col & (BLOCK - 1))
    pick = (inside & (at == wanted)).astype(F32).astype(BF16)
    patches = dot(pick, patch_rows[...]).astype(BF16)
    chunk = 512
    chunks = norm_rows.shape[0] // chunk

    def per_row(index, carry):
        rows = tile_b[pl.ds(pl.multiple_of(index * LANES, LANES), LANES), :]

        def per_chunk(step, state):
            best, mass = state
            block = norm_rows[pl.ds(pl.multiple_of(step * chunk, chunk), chunk), :]
            scores = dot(rows, block, NT) * sz.scale
            fresh = jnp.maximum(best, jnp.max(scores, axis=1, keepdims=True))
            mass = mass * jnp.exp(best - fresh) + jnp.sum(jnp.exp(scores - fresh), axis=1, keepdims=True)
            return fresh, mass

        if chunks == 1:
            scores = dot(rows, norm_rows[...], NT) * sz.scale
            best = jnp.max(scores, axis=1, keepdims=True)
            mass = jnp.sum(jnp.exp(scores - best), axis=1, keepdims=True)
        else:
            start = jnp.full((LANES, 1), -jnp.inf, F32), jnp.zeros((LANES, 1), F32)
            best, mass = lax.fori_loop(0, chunks, per_chunk, start)
        norm_a = best + jnp.log(mass)
        near = dot(rows, patches, NT) * sz.scale
        place = pl.ds(pl.multiple_of(index * LANES, LANES), LANES)
        own_ref[place, :] = near
        u_ref[place, :] = 2.0 * near - norm_a + sz.offset
        return carry

    lax.fori_loop(0, sz.halo_b, per_row, 0)
    own = own_ref[2 * LANES : (2 + sz.rows_b) * LANES, :]
    best = jnp.max(own, axis=0, keepdims=True)
    mass = jnp.sum(jnp.exp(own - best), axis=0, keepdims=True)
    part_ref[...] = jnp.concatenate(
        [best, mass, jnp.zeros((6, sz.lanes_in), F32)], axis=0
    )


def scores_kernel_direct(sz, rank_ref, norm_rows, patch_rows, tile_b, u_ref, part_ref, own_ref):
    scores_body(sz, rank_ref, norm_rows, patch_rows, tile_b, u_ref, part_ref, own_ref)


def scores_kernel_pieces(
    sz, count, rank_ref, own_piece, core_piece, cross_piece, diag_piece,
    u_ref, part_ref, own_a_ref, own_b_ref,
    norm_rows, patch_rows, tile_b, near_ref,
):
    row_rank, col_rank = rank_ref[0], rank_ref[1]
    cells = sz.rows_a * BLOCK
    cols = sz.width_b // count
    pieces = ((own_piece, 0), (core_piece, 1), (diag_piece, 2), (cross_piece, 3))
    for order, (piece, flip) in enumerate(pieces):
        norm_rows[order * count * cells : (order + 1) * count * cells, :] = piece[
            :, 0:cells, :
        ].reshape(count * cells, sz.channels)
        block = col_rank ^ flip
        for step in range(3):
            where_from = jnp.clip(row_rank - 1 + step, 0, count - 1)
            start = pl.multiple_of(block * (3 * cells) + step * cells, cells)
            patch_rows[pl.ds(start, cells), :] = piece[where_from, 0:cells, :]
        start = pl.multiple_of(block * cells, cells)
        own_a_ref[pl.ds(start, cells), :] = piece[row_rank, 0:cells, :]
    width = sz.width_b
    for row in range(sz.rows_b):
        rows = own_piece[:, cells + row * cols : cells + (row + 1) * cols, :].reshape(width, sz.channels)
        tile_b[(2 + row) * width : (3 + row) * width, :] = rows
        own_b_ref[row * width : (row + 1) * width, :] = rows
    odd = col_rank & 1
    far = (2 + sz.rows_b) * width
    for piece, base in ((core_piece, (1 - odd) * far), (cross_piece, odd * far)):
        for row in range(2):
            rows = piece[:, cells + row * cols : cells + (row + 1) * cols, :].reshape(width, sz.channels)
            tile_b[pl.ds(pl.multiple_of(base + row * width, width), width), :] = rows
    scores_body(sz, rank_ref, norm_rows, patch_rows, tile_b, u_ref, part_ref, near_ref)


def softplus(values):
    return jnp.maximum(values, 0.0) + jnp.log1p(jnp.exp(-jnp.abs(values)))


def refine_kernel(sz, parts, split, rank_ref, u_ref, *refs):
    part_refs = refs[:parts]
    t_in, t_out, bias_row, own_a, own_b = refs[parts : parts + 5]
    outs = refs[parts + 5 : -4]
    refined_ref, sums_a_ref = outs[0], outs[1]
    x_ref, mid_ref, share_ref, stat_ref = refs[-4:]
    row_rank, col_rank = rank_ref[0], rank_ref[1]
    last = sz.grid_b // sz.rows_b - 1
    tops, masses = [], []
    for ref in part_refs:
        for at in range(ref.shape[0] // 8):
            tops.append(ref[at * 8 : at * 8 + 1, :])
            masses.append(ref[at * 8 + 1 : at * 8 + 2, :])
    top = functools.reduce(jnp.maximum, tops)
    mass = sum(m * jnp.exp(t - top) for t, m in zip(tops, masses))
    norm_b = top + jnp.log(mass)

    row, _, inside = patch_lanes(sz, (1, sz.lanes_in), 1)
    row = row + row_rank * sz.rows_a - 2
    inside = inside & (row >= 0) & (row < sz.grid_a)
    lane = iota((LANES, LANES), 1)
    line = iota((LANES, LANES), 0)
    low = lane < HALF
    low_down = low & (line > 0)
    low_up = low & (line < LANES - 1)

    def place_matched(index, carry):
        place = pl.ds(pl.multiple_of(index * LANES, LANES), LANES)
        matched = softplus(u_ref[place, :] - norm_b)
        matched = jnp.where(inside, matched, 0.0)
        for pair in range(sz.blocks // 2):
            here = matched[:, pair * LANES : (pair + 1) * LANES]
            turned = pltpu.roll(here, HALF, 1)
            for side, (one, two) in enumerate(((here, turned), (turned, here))):
                block = pair * 2 + side
                first = jnp.where(low, jnp.where(low_down, pltpu.roll(one, 1, 0), 0.0), two)
                second = jnp.where(low_up, pltpu.roll(one, LANES - 1, 0), 0.0)
                x_ref[block, place, 0:LANES] = first.astype(BF16)
                x_ref[block, place, LANES : 2 * LANES] = second.astype(BF16)
        return carry

    lax.fori_loop(0, sz.halo_b, place_matched, 0)
    edge = 2 * LANES
    far = (2 + sz.rows_b) * LANES

    @pl.when(col_rank == 0)
    def _():
        x_ref[:, 0:edge, :] = jnp.zeros((sz.blocks, edge, 2 * LANES), BF16)

    @pl.when(col_rank == last)
    def _():
        x_ref[:, far : far + edge, :] = jnp.zeros((sz.blocks, edge, 2 * LANES), BF16)

    rows_mid = sz.mid_b * LANES
    lane = iota((1, sz.lanes_mid), 1)
    row = (lane // BLOCK) % sz.mid_a + row_rank * sz.rows_a - 1
    inside_mid = (row >= 0) & (row < sz.grid_a)
    bias = bias_row[...]
    for block in range(sz.blocks):
        total = bias
        for three in range(3):
            total = total + dot(
                x_ref[block, three * LANES : three * LANES + rows_mid, :],
                t_in[three * 4 * HALF : (three + 1) * 4 * HALF, :],
            )
        hidden = jnp.where(inside_mid, jnp.maximum(total, 0.0), 0.0)
        mid_ref[:, block * sz.lanes_mid : (block + 1) * sz.lanes_mid] = hidden.astype(BF16)
    wide = sz.blocks * sz.lanes_mid

    @pl.when(col_rank == 0)
    def _():
        mid_ref[0:LANES, :] = jnp.zeros((LANES, wide), BF16)

    @pl.when(col_rank == last)
    def _():
        mid_ref[rows_mid - LANES : rows_mid, :] = jnp.zeros((LANES, wide), BF16)

    spread = 0.0
    for three in range(3):
        spread = spread + dot(
            mid_ref[three * LANES : three * LANES + sz.cells_b, :],
            t_out[three * wide : (three + 1) * wide, :],
        )
    best_b = None
    for row in range(sz.rows_b):
        left = spread[row * LANES : (row + 1) * LANES, 0:LANES]
        right = spread[row * LANES : (row + 1) * LANES, LANES : 2 * LANES]
        filtered = (
            jnp.where(line > 0, pltpu.roll(left, 1, 0), 0.0)
            + pltpu.roll(left, HALF, 1)
            + jnp.where(line < LANES - 1, pltpu.roll(right, LANES - 1, 0), 0.0)
        )
        filtered = jnp.maximum(filtered, 0.0).T[0:HALF, :]
        scores = dot(own_a[...], own_b[row * LANES : (row + 1) * LANES, :], NT) * sz.scale
        refined = scores + filtered
        refined_ref[:, row * LANES : (row + 1) * LANES] = refined
        top = jnp.max(refined, axis=0, keepdims=True)
        sums_a_ref[row : row + 1, :] = top
        sums_a_ref[sz.rows_b + row : sz.rows_b + row + 1, :] = jnp.sum(
            jnp.exp(refined - top), axis=0, keepdims=True
        )
        best = jnp.max(refined, axis=1, keepdims=True)
        best_b = best if best_b is None else jnp.maximum(best_b, best)
    weights = jnp.exp(refined_ref[...] - best_b)
    total_b = jnp.sum(weights, axis=1, keepdims=True)
    high = weights.astype(BF16)
    rest = (weights - high.astype(F32)).astype(BF16)
    share = dot(high, own_b[...]) + dot(rest, own_b[...])
    lane = iota((HALF, LANES), 1)
    stats = jnp.where(lane < HALF, best_b, total_b)
    if not split:
        outs[2][...] = share
        outs[3][...] = stats
        return
    share_ref[...] = share
    cells = sz.rows_a * BLOCK
    for flip in range(4):
        out = outs[2 + flip]
        start = pl.multiple_of((col_rank ^ flip) * cells, cells)
        out[0:cells, :] = share_ref[pl.ds(start, cells), :]
        out[cells:, 0:LANES] = stats[0 : HALF // 2, :]
        out[cells:, LANES:] = stats[HALF // 2 :, :]


def finish_kernel(sz, count, rank_ref, refined_ref, sums_ref, own, core, diag, cross, out_ref, warped_ref, stat_ref):
    col_rank = rank_ref[1]
    cells = sz.rows_a * BLOCK
    lane = iota((HALF, LANES), 1)
    tops, masses = [], []
    for at, ref in enumerate((own, core, diag, cross)):
        stats = jnp.concatenate([ref[cells:, 0:LANES], ref[cells:, LANES:]], axis=0)
        turned = pltpu.roll(stats, HALF, 1)
        tops.append(jnp.where(lane < HALF, stats, turned))
        masses.append(jnp.where(lane < HALF, turned, stats))
        stat_ref[at] = tops[-1]
    top = functools.reduce(jnp.maximum, tops)
    norm_b = top + jnp.log(sum(m * jnp.exp(t - top) for t, m in zip(tops, masses)))
    stat_ref[4] = norm_b
    mine = pl.ds(pl.multiple_of(col_rank * cells, cells), cells)
    norm_mine = stat_ref[4, mine, :]
    warped = 0.0
    for at, ref in enumerate((own, core, diag, cross)):
        factor = jnp.exp(stat_ref[at, mine, :] - norm_mine)
        warped = warped + ref[0:cells, :] * jnp.concatenate(
            [factor] * (sz.channels // LANES), axis=1
        )
    warped_ref[...] = warped.reshape(sz.rows_a, BLOCK, sz.channels)
    tops = [sums_ref[at * 8 : at * 8 + sz.rows_b, :] for at in range(count)]
    masses = [sums_ref[at * 8 + sz.rows_b : at * 8 + 2 * sz.rows_b, :] for at in range(count)]
    top = functools.reduce(jnp.maximum, tops)
    norm_a = top + jnp.log(sum(m * jnp.exp(t - top) for t, m in zip(tops, masses)))
    for row in range(sz.rows_b):
        values = (
            2.0 * refined_ref[:, row * LANES : (row + 1) * LANES]
            - norm_a[row : row + 1, :]
            - norm_b
            + sz.offset
        )
        for block in range(sz.blocks):
            for high in range(sz.rows_a):
                start = block * cells + high * BLOCK
                out_ref[high, block * BLOCK : (block + 1) * BLOCK, row, :] = values[start : start + BLOCK, :]


def call(kernel, name, outs, scratch, *args):
    return pl.pallas_call(
        kernel,
        out_shape=outs,
        in_specs=[smem_spec()] + vmem_specs(len(args) - 1),
        out_specs=tuple(vmem_specs(len(outs))),
        scratch_shapes=scratch,
        name=name,
    )(*args)


def refine_call(sz, parts, split, *args):
    shape = jax.ShapeDtypeStruct
    cells = sz.rows_a * BLOCK
    outs = [shape((HALF, sz.cells_b), F32), shape((8, LANES), F32)]
    if split:
        outs += [shape((cells + HALF // 2, 2 * LANES), F32)] * 4
    else:
        outs += [shape((HALF, sz.channels), F32), shape((HALF, LANES), F32)]
    scratch = [
        pltpu.VMEM((sz.blocks, sz.halo_b * LANES, 2 * LANES), BF16),
        pltpu.VMEM((sz.mid_b * LANES, sz.blocks * sz.lanes_mid), BF16),
        pltpu.VMEM((HALF, sz.channels), F32),
        pltpu.VMEM((HALF, LANES), F32),
    ]
    return call(functools.partial(refine_kernel, sz, parts, split), "refine", tuple(outs), scratch, *args)


def swap(value, flip, count):
    return lax.ppermute(value, "ba", [(at, at ^ flip) for at in range(count)])


def sizes_of(features_a, features_b, conv_in):
    rows_a, cols_a, channels = features_a.shape
    rows_b, cols_b, _ = features_b.shape
    count_a, count_b = lax.axis_size("aa"), lax.axis_size("ba")
    return Sizes(
        rows_a, cols_a * count_b, rows_b, cols_b * count_a, channels, conv_in.shape[0],
        rows_a * count_a, rows_b * count_b,
    )


def local_four(features_a, features_b, conv_in, bias_in, conv_out):
    sz = sizes_of(features_a, features_b, conv_in)
    count = lax.axis_size("aa")
    shape = jax.ShapeDtypeStruct
    row_rank, col_rank = lax.axis_index("aa"), lax.axis_index("ba")
    rank = jnp.stack([row_rank, col_rank]).astype(jnp.int32)
    cells = sz.rows_a * BLOCK
    cols = features_b.shape[1]
    mine = jnp.concatenate(
        [features_a.reshape(cells, sz.channels), features_b.reshape(-1, sz.channels)], axis=0
    )
    spread = jnp.broadcast_to(mine[None], (count,) + mine.shape)
    own = lax.all_to_all(spread, "aa", 0, 0, tiled=True)
    rows_here = own[:, 0:cells]
    first = own[:, cells : cells + 2 * cols]
    final = own[:, cells + (sz.rows_b - 2) * cols :]
    odd = (col_rank & 1) == 1
    core = swap(jnp.concatenate([rows_here, jnp.where(odd, first, final)], axis=1), 1, 4)
    cross = swap(jnp.concatenate([rows_here, jnp.where(odd, final, first)], axis=1), 3, 4)
    diag = swap(rows_here, 2, 4)
    t_in, t_out, bias_row = build_taps(sz, conv_in, bias_in, conv_out)
    u, part, own_a, own_b = call(
        functools.partial(scores_kernel_pieces, sz, count),
        "scores",
        (
            shape((sz.halo_b * LANES, sz.lanes_in), F32),
            shape((8, sz.lanes_in), F32),
            shape((HALF, sz.channels), BF16),
            shape((sz.cells_b, sz.channels), BF16),
        ),
        [
            pltpu.VMEM((sz.grid_a * sz.width_a, sz.channels), BF16),
            pltpu.VMEM((sz.halo_a * sz.width_a, sz.channels), BF16),
            pltpu.VMEM((sz.halo_b * LANES, sz.channels), BF16),
            pltpu.VMEM((sz.halo_b * LANES, sz.lanes_in), F32),
        ],
        rank, own, core, cross, diag,
    )
    others = [swap(part, flip, 4) for flip in (1, 3, 2)]
    refined, sums_a, *bundles = refine_call(
        sz, 4, True, rank, u, part, *others, t_in, t_out, bias_row, own_a, own_b
    )
    moved = [swap(bundles[flip], flip, 4) for flip in (1, 3, 2)]
    sums = jnp.broadcast_to(sums_a[None], (count,) + sums_a.shape)
    sums = lax.all_to_all(sums, "aa", 0, 0, tiled=True).reshape(count * 8, LANES)
    return call(
        functools.partial(finish_kernel, sz, count),
        "finish",
        (
            shape((sz.rows_a, sz.width_a, sz.rows_b, LANES), F32),
            shape((sz.rows_a, BLOCK, sz.channels), F32),
        ),
        [pltpu.VMEM((5, HALF, LANES), F32)],
        rank, refined, sums, bundles[0], moved[0], moved[2], moved[1],
    )


def local_any(features_a, features_b, conv_in, bias_in, conv_out):
    sz = sizes_of(features_a, features_b, conv_in)
    count_b = lax.axis_size("ba")
    shape = jax.ShapeDtypeStruct
    row_rank, col_rank = lax.axis_index("aa"), lax.axis_index("ba")
    rank = jnp.stack([row_rank, col_rank]).astype(jnp.int32)
    channels = sz.channels
    rows_a = lax.all_gather(features_a, "ba", axis=1, tiled=True)
    all_a = lax.all_gather(rows_a, "aa", axis=0, tiled=True)
    around = lax.dynamic_slice_in_dim(
        jnp.pad(all_a, ((2, 2), (0, 0), (0, 0))), row_rank * sz.rows_a, sz.halo_a, axis=0
    )

    def blocked(rows):
        split = rows.reshape(rows.shape[0], sz.blocks, BLOCK, channels)
        return jnp.transpose(split, (1, 0, 2, 3)).reshape(-1, channels)

    rows_b = lax.all_gather(features_b, "aa", axis=1, tiled=True)
    ends = count_b - 1
    before = lax.ppermute(rows_b[-2:], "ba", [(at, at + 1) for at in range(ends)])
    after = lax.ppermute(rows_b[:2], "ba", [(at + 1, at) for at in range(ends)])
    tile_b = jnp.concatenate([before, rows_b, after], axis=0).reshape(-1, channels)
    t_in, t_out, bias_row = build_taps(sz, conv_in, bias_in, conv_out)
    u, part = call(
        functools.partial(scores_kernel_direct, sz),
        "scores",
        (shape((sz.halo_b * LANES, sz.lanes_in), F32), shape((8, sz.lanes_in), F32)),
        [pltpu.VMEM((sz.halo_b * LANES, sz.lanes_in), F32)],
        rank, all_a.reshape(-1, channels), blocked(around), tile_b,
    )
    parts = lax.all_gather(part, "ba", axis=0, tiled=True)
    refined, sums_a, share, stats = refine_call(
        sz, 1, False, rank, u, parts, t_in, t_out, bias_row, blocked(rows_a), rows_b.reshape(-1, channels)
    )
    top, mass = stats[:, 0], stats[:, HALF]
    best = lax.pmax(top, "ba")
    norm_b = best + jnp.log(lax.psum(mass * jnp.exp(top - best), "ba"))

    def unblocked(rows):
        split = rows.reshape((sz.blocks, sz.rows_a, BLOCK) + rows.shape[1:])
        return jnp.swapaxes(split, 0, 1).reshape((sz.rows_a, sz.width_a) + rows.shape[1:])

    share = unblocked(share * jnp.exp(top - norm_b)[:, None])
    warped = lax.psum_scatter(share, "ba", scatter_dimension=1, tiled=True)
    top, mass = sums_a[: sz.rows_b], sums_a[sz.rows_b : 2 * sz.rows_b]
    best = lax.pmax(top, "aa")
    norm_a = best + jnp.log(lax.psum(mass * jnp.exp(top - best), "aa"))
    refined = refined.reshape(HALF, sz.rows_b, LANES)
    mutual = 2.0 * refined - norm_a - norm_b[:, None, None] + sz.offset
    return unblocked(mutual), warped


def local(features_a, features_b, *rest):
    suits = lax.axis_size("ba") == 4 and features_a.shape[1] == BLOCK and features_b.shape[1] % 16 == 0
    return (local_four if suits else local_any)(features_a, features_b, *rest)


def solution(mesh):
    placed = (P("aa", "ba", None), P("ba", "aa", None), P(), P(), P())
    return jax.shard_map(
        local,
        mesh=mesh,
        in_specs=placed,
        out_specs=(P("aa", None, "ba", None), P("aa", "ba", None)),
        check_vma=False,
    )
```

time: 319 us -> 66.8 us (0.21)
  blocking collectives: 140 us -> 0 us
  local copies, waits for them, and re-layouts: 65 us -> 6.73 us
  other arithmetic: 55 us -> 1.41 us
  Pallas kernels: 0 us -> 19.3 us
  between operations: 14.9 us -> 0.75 us
    pmax x4 -> x0, blocking collectives: 54.2 us -> none  [the longest x2 40.7 us: dual_norms(): top_a = lax.pmax(jnp.max(values, axis=(0, 1)), 'aa')]
    slice x87 -> x1, local copies, waits for them, and re-layouts: 51.2 us -> 0.01 us  [local_four(): rows_here = own[:, 0:cells]]
    psum x4 -> x0, blocking collectives: 48.1 us -> none  [the longest x2 34.3 us: dual_norms(): mass_a = lax.psum(jnp.sum(jnp.exp(values - top_a), axis=(0, 1)), 'aa')]
    all_gather x2 -> x0, blocking collectives: 38.2 us -> none  [the longest x1 32.8 us: local(): rows_b = lax.all_gather(features_b, 'aa', axis=1, tiled=True)]
    reduce_sum x14 -> x0, other arithmetic: 34.3 us -> none  [the longest x11 33.8 us: reduce_taps(): jnp.sum(kernel[:, offsets[0], offsets[1], offsets[2], offsets[3]].reshape...]
    pallas_call x0 -> x4, Pallas kernels: none -> 19.3 us  [the longest x3 16.1 us: call(): pl.pallas_call(kernel, out_shape=outs, in_specs=[smem_spec()] + vmem_spec...]
    ppermute x8 -> x9, starting transfers between devices: 19.3 us -> 6.19 us  [swap(): return lax.ppermute(value, 'ba', [(at, at ^ flip) for at in range(count)])]
    mul x10 -> x0, local copies, waits for them, and re-layouts: 12.9 us -> none  [the longest x5 7.37 us: spread_taps(): kernel[:, offsets[0], offsets[1], offsets[2], offsets[3]]]
  transfers between devices with their start and end apart: 9 -> 11, of which waited for: 2 -> 5; matrix products, arithmetic and copies ran while one was open for 5% -> 4% of each run, Pallas kernels for 0% -> 5%
where the time goes in v1:
time: 66.8 us; the launch traced here: 66.3 us
  waiting for transfers between devices  21 us (31%)
  Pallas kernels  19.3 us (29%)
  starting transfers between devices  17.1 us (26%)
  local copies, waits for them, and re-layouts  6.73 us (10%)
  other arithmetic  1.41 us (2%)
  between operations  0.75 us (1%)
    pallas_call x3, Pallas kernels, call(): pl.pallas_call(kernel, out_shape=outs, in_specs=[smem_spec()] + vmem_spec...  16.1 us
    all_to_all x1, waiting for transfers between devices, local_four(): own = lax.all_to_all(spread, 'aa', 0, 0, tiled=True)  10.3 us
    ppermute x9, waiting for transfers between devices, swap(): return lax.ppermute(value, 'ba', [(at, at ^ flip) for at in range(count)])  8.96 us
    all_to_all x1, starting transfers between devices, local_four(): own = lax.all_to_all(spread, 'aa', 0, 0, tiled=True)  7.28 us
    ppermute x9, starting transfers between devices, swap(): return lax.ppermute(value, 'ba', [(at, at ^ flip) for at in range(count)])  6.19 us
    all_to_all x1, starting transfers between devices, local_four(): lax.all_to_all(sums, 'aa', 0, 0, tiled=True).reshape(count * 8, LANES)  3.62 us
    pallas_call x1, Pallas kernels, build_taps(): pl.pallas_call(functools.partial(taps_kernel, sz), out_shape=(jax.ShapeDt...  3.18 us
    unnamed x28, local copies, waits for them, and re-layouts  2.57 us
  transfers between devices with their start and end apart: 11, of which 5 were waited for; matrix products, arithmetic and copies ran while one was open for 4% of the time, Pallas kernels for 5%

profile of v1, /device:TPU:0, one launch (start us, length us, event | category | flops | bytes accessed | tf_op | source)
XLA Modules:
  0.0 66.3 jit_solution(3412545094832779901)
XLA Ops:
  0.6 0.8 %pad_maximum_fusion.2 = bf16[80,256]{1,0:T(8,128)(2,1)S(1)} fusion(bf16[64,256]{1,0:T(8,128)(2,1)} %bitcast.13, bf16[16,256]{1,0:T(8,128)(2,1)} %bitcast.14), kind=kLoop, calls=%fused_computation.4 | loop fusion | flops 81920 | bytes 81920 | tf_op jit(solution)/shard_map/concatenate | solution.py:461
  1.4 0.0 copy-start.6
  1.4 0.7 %broadcast_in_dim.4 = bf16[8,80,256]{2,1,0:T(8,128)(2,1)} broadcast(bf16[80,256]{1,0:T(8,128)(2,1)S(1)} %pad_maximum_fusion.2), dimensions={1,2} | broadcast | bytes 368640 | tf_op jit(solution)/shard_map/broadcast_in_dim | solution.py:464
  2.2 7.3 %all-to-all-start = ((bf16[8,80,256]{2,1,0:T(8,128)(2,1)}), bf16[8,80,256]{2,1,0:T(8,128)(2,1)S(1)}, u32[]{:S(2)}, u32[]{:S(2)}) async-start(bf16[8,80,256]{2,1,0:T(8,128)(2,1)} %broadcast_in_dim.4), calls=%async_computation | async-start | bytes 655360 | tf_op jit(solution)/shard_map/all_to_all | solution.py:465
  9.4 10.3 %all-to-all-done.own_piece = bf16[8,80,256]{2,1,0:T(8,128)(2,1)S(1)} async-done(((bf16[8,80,256]{2,1,0:T(8,128)(2,1)}), bf16[8,80,256]{2,1,0:T(8,128)(2,1)S(1)}, u32[]{:S(2)}, u32[]{:S(2)}) %all-to-all-start) | async-done | bytes 327712 | tf_op jit(solution)/shard_map/all_to_all | solution.py:465
  19.8 0.1 collective-permute-start.1
  19.9 1.6 %collective-permute-start = (bf16[8,48,256]{2,1,0:T(8,128)(2,1)S(1)}, bf16[8,48,256]{2,1,0:T(8,128)(2,1)S(1)}, u32[]{:S(2)}, u32[]{:S(2)}) collective-permute-start(bf16[8,48,256]{2,1,0:T(8,128)(2,1)S(1)} %get-tuple-element.31), channel_id=1, source_target_pairs={{0,1},{1,0},{2,3},{3,2},{4,5},{5,4},{6,7},{7,6},{8,9},{9,8},{10,11... | collective-permute-start | bytes 589832 | tf_op jit(solution)/shard_map/ppermute | solution.py:440
  21.5 0.5 collective-permute-start.2
  22.0 0.6 pad_add_fusion.rank_ref
  22.6 5.9 %collective-permute-done.2.diag_piece = bf16[8,16,256]{2,1,0:T(8,128)(2,1)S(1)} collective-permute-done((bf16[8,16,256]{2,1,0:T(8,128)(2,1)S(1)}, bf16[8,16,256]{2,1,0:T(8,128)(2,1)S(1)}, u32[]{:S(2)}, u32[]{:S(2)}) %collective-permute-start.2) | collective-permute-done | bytes 65568 | tf_op jit(solution)/shard_map/ppermute | solution.py:440
  28.5 0.0 collective-permute-done.1.cross_piece
  28.5 0.0 collective-permute-done.core_piece
  28.5 0.0 copy-done
  28.5 0.6 copy-done.4
  29.1 0.1 copy-done.1
  29.2 0.7 %copy-done.2 = bf16[8,48,256]{2,1,0:T(8,128)(2,1)} copy-done((bf16[8,48,256]{2,1,0:T(8,128)(2,1)}, bf16[8,48,256]{2,1,0:T(8,128)(2,1)S(1)}, u32[]{:S(2)}) %copy-start.2) | copy-done | bytes 196632
  29.9 5.7 %scores.1 = (f32[1024,256]{1,0:T(8,128)}, f32[8,256]{1,0:T(8,128)}, bf16[64,256]{1,0:T(8,128)(2,1)}, bf16[512,256]{1,0:T(8,128)(2,1)}) custom-call(s32[2]{0:T(128)} %pad_add_fusion.rank_ref, bf16[8,80,256]{2,1,0:T(8,128)(2,1)} %copy-done, bf16[8,48,256]{2,1,0:T(8,128)(2,1)} %copy-done.2, bf16[8,48,256]{2,1,0:T(8,128)(2,1)} %copy-done.1, ...), custom_call_target="tpu_custom_call" | custom-call | tf_op jit(solution)/shard_map/scores/pallas_call | solution.py:412
  35.6 0.0 collective-permute-start.5
  35.6 1.4 %collective-permute-start.4 = (f32[8,256]{1,0:T(8,128)}, f32[8,256]{1,0:T(8,128)S(1)}, u32[]{:S(2)}, u32[]{:S(2)}) collective-permute-start(f32[8,256]{1,0:T(8,128)} %get-tuple-element.16.refs_0_), channel_id=1, source_target_pairs={{0,3},{1,2},{2,1},{3,0},{4,7},{5,6},{6,5},{7,4},{8,11},{9,10},{10,... | collective-permute-start | bytes 24584 | tf_op jit(solution)/shard_map/ppermute | solution.py:440
  37.0 0.8 %collective-permute-start.3 = (f32[8,256]{1,0:T(8,128)}, f32[8,256]{1,0:T(8,128)S(1)}, u32[]{:S(2)}, u32[]{:S(2)}) collective-permute-start(f32[8,256]{1,0:T(8,128)} %get-tuple-element.16.refs_0_), channel_id=1, source_target_pairs={{0,1},{1,0},{2,3},{3,2},{4,5},{5,4},{6,7},{7,6},{8,9},{9,8},{10,11... | collective-permute-start | bytes 24584 | tf_op jit(solution)/shard_map/ppermute | solution.py:440
  37.7 0.0 copy-done.13
  37.7 0.7 %copy.11.bias_ref = f32[8,1]{1,0:T(8,128)} copy(f32[8,1]{0,1:T(1,128)S(1)} %bitcast.15) | data formatting | bytes 64 | tf_op jit(solution)/shard_map/reshape | solution.py:157
  38.4 0.0 copy-done.5
  38.4 0.6 reshape.26.w_in_ref
  39.0 0.1 reshape.27
  39.1 0.1 copy.10
  39.2 0.6 pad.4.w_out_ref
  39.9 3.2 %taps.1 = (bf16[768,256]{1,0:T(8,128)(2,1)}, bf16[3072,256]{1,0:T(8,128)(2,1)}, f32[1,256]{1,0:T(1,128)}) custom-call(f32[81,8]{1,0:T(8,128)} %reshape.26.w_in_ref, f32[72,16]{1,0:T(8,128)} %pad.4.w_out_ref, f32[8,1]{1,0:T(8,128)} %copy.11.bias_ref), custom_call_target="tpu_custom_call" | custom-call | tf_op jit(solution)/shard_map/taps/pallas_call | solution.py:143
  43.0 0.0 collective-permute-done.5.refs_3_
  43.0 0.0 collective-permute-done.4.refs_2_
  43.1 0.0 collective-permute-done.3.refs_1_
  43.1 0.0 copy-start.12
  43.1 0.6 copy-done.10
  43.6 0.0 copy-done.11
  43.6 0.0 copy-done.12
  43.7 8.6 %refine.1 = (f32[64,512]{1,0:T(8,128)}, f32[8,128]{1,0:T(8,128)}, f32[48,256]{1,0:T(8,128)}, f32[48,256]{1,0:T(8,128)}, f32[48,256]{1,0:T(8,128)}, /*index=5*/f32[48,256]{1,0:T(8,128)}) custom-call(s32[2]{0:T(128)} %pad_add_fusion.rank_ref, f32[1024,256]{1,0:T(8,128)} %get-tuple-element.15.u_ref, f32[8,256]{1,0:T(8,128)} %get-tuple-element.16.refs_0_, ...), custom_call_target="tpu_custom_call" | custom-call | tf_op jit(solution)/shard_map/refine/pallas_call | solution.py:412
  52.2 1.3 %broadcast_in_dim.5 = f32[8,8,128]{2,1,0:T(8,128)} broadcast(f32[8,128]{1,0:T(8,128)} %get-tuple-element.23), dimensions={1,2} | broadcast | bytes 36864 | tf_op jit(solution)/shard_map/broadcast_in_dim | solution.py:496
  53.5 3.6 %all-to-all-start.1 = ((f32[8,8,128]{2,1,0:T(8,128)}), f32[8,8,128]{2,1,0:T(8,128)S(1)}, u32[]{:S(2)}, u32[]{:S(2)}) async-start(f32[8,8,128]{2,1,0:T(8,128)} %broadcast_in_dim.5), calls=%async_computation.1 | async-start | bytes 65536 | tf_op jit(solution)/shard_map/all_to_all | solution.py:497
  57.1 0.0 collective-permute-start.6
  57.1 0.7 %collective-permute-start.7 = (f32[48,256]{1,0:T(8,128)}, f32[48,256]{1,0:T(8,128)S(1)}, u32[]{:S(2)}, u32[]{:S(2)}) collective-permute-start(f32[48,256]{1,0:T(8,128)} %get-tuple-element.26), channel_id=1, source_target_pairs={{0,2},{1,3},{2,0},{3,1},{4,6},{5,7},{6,4},{7,5},{8,10},{9,11},{10,... | collective-permute-start | bytes 147464 | tf_op jit(solution)/shard_map/ppermute | solution.py:440
  57.8 1.2 %collective-permute-start.8 = (f32[48,256]{1,0:T(8,128)}, f32[48,256]{1,0:T(8,128)S(1)}, u32[]{:S(2)}, u32[]{:S(2)}) collective-permute-start(f32[48,256]{1,0:T(8,128)} %get-tuple-element.27), channel_id=1, source_target_pairs={{0,3},{1,2},{2,1},{3,0},{4,7},{5,6},{6,5},{7,4},{8,11},{9,10},{10,... | collective-permute-start | bytes 147464 | tf_op jit(solution)/shard_map/ppermute | solution.py:440
  59.0 0.0 collective-permute-done.6.core
  59.0 3.0 %collective-permute-done.7.diag = f32[48,256]{1,0:T(8,128)S(1)} collective-permute-done((f32[48,256]{1,0:T(8,128)}, f32[48,256]{1,0:T(8,128)S(1)}, u32[]{:S(2)}, u32[]{:S(2)}) %collective-permute-start.7) | collective-permute-done | bytes 49184 | tf_op jit(solution)/shard_map/ppermute | solution.py:440
  62.0 0.1 collective-permute-done.8.cross
  62.1 1.7 %all-to-all-done.1 = f32[8,8,128]{2,1,0:T(8,128)S(1)} async-done(((f32[8,8,128]{2,1,0:T(8,128)}), f32[8,8,128]{2,1,0:T(8,128)S(1)}, u32[]{:S(2)}, u32[]{:S(2)}) %all-to-all-start.1) | async-done | bytes 32800 | tf_op jit(solution)/shard_map/all_to_all | solution.py:497
  63.8 0.0 copy-done.8
  63.8 0.6 copy-done.3
  64.4 1.9 %finish.1 = (f32[2,32,4,128]{3,2,1,0:T(4,128)}, f32[2,8,256]{2,1,0:T(8,128)}) custom-call(s32[2]{0:T(128)} %pad_add_fusion.rank_ref, f32[64,512]{1,0:T(8,128)} %get-tuple-element.22.refined_ref, f32[64,128]{1,0:T(8,128)} %bitcast.10, f32[48,256]{1,0:T(8,128)} %get-tuple-element.24.own, f32[48,256]{1,0:T(8,128)} %copy-done.7, f32[48,256]{1,0:T(8,128)} %copy-done.8, ...), custom_call_target="tpu_custom_call" | custom-call | tf_op jit(solution)/shard_map/finish/pallas_call | solution.py:412
  (19 shorter events, 0.1 us)
Async XLA Ops:
  1.4 36.3 %copy-start.13 = (f32[8]{0:T(128)S(1)}, f32[8]{0:T(128)}, u32[]{:S(2)}) copy-start(f32[8]{0:T(128)} %param.8) | copy-start | bytes 100
  1.4 37.0 %copy-start.5 = (f32[8,3,3,3,3]{0,4,3,2,1:T(4,128)S(1)}, f32[8,3,3,3,3]{0,4,3,2,1:T(4,128)}, u32[]{:S(2)}) copy-start(f32[8,3,3,3,3]{0,4,3,2,1:T(4,128)} %param.7) | copy-start | bytes 7780
  1.4 37.6 %copy-start.6 = (f32[8,3,3,3,3]{0,4,3,2,1:T(4,128)S(1)}, f32[8,3,3,3,3]{0,4,3,2,1:T(4,128)}, u32[]{:S(2)}) copy-start(f32[8,3,3,3,3]{0,4,3,2,1:T(4,128)} %param.9) | copy-start | bytes 7780
  2.2 17.6 %all-to-all-start = ((bf16[8,80,256]{2,1,0:T(8,128)(2,1)}), bf16[8,80,256]{2,1,0:T(8,128)(2,1)S(1)}, u32[]{:S(2)}, u32[]{:S(2)}) async-start(bf16[8,80,256]{2,1,0:T(8,128)(2,1)} %broadcast_in_dim.4), calls=%async_computation | async-start | bytes 655360 | tf_op jit(solution)/shard_map/all_to_all | solution.py:465
  19.7 8.8 %copy-start = (bf16[8,80,256]{2,1,0:T(8,128)(2,1)}, bf16[8,80,256]{2,1,0:T(8,128)(2,1)S(1)}, u32[]{:S(2)}) copy-start(bf16[8,80,256]{2,1,0:T(8,128)(2,1)S(1)} %all-to-all-done.own_piece) | copy-start | bytes 983044
  19.8 8.7 %collective-permute-start.1 = (bf16[8,48,256]{2,1,0:T(8,128)(2,1)S(1)}, bf16[8,48,256]{2,1,0:T(8,128)(2,1)S(1)}, u32[]{:S(2)}, u32[]{:S(2)}) collective-permute-start(bf16[8,48,256]{2,1,0:T(8,128)(2,1)S(1)} %get-tuple-element.30), channel_id=1, source_target_pairs={{0,3},{1,2},{2,1},{3,0},{4,7},{5,6},{6,5},{7,4},{8,11},{9,10},{10,... | collective-permute-start | bytes 589832 | tf_op jit(solution)/shard_map/ppermute | solution.py:440
  19.9 8.6 %collective-permute-start = (bf16[8,48,256]{2,1,0:T(8,128)(2,1)S(1)}, bf16[8,48,256]{2,1,0:T(8,128)(2,1)S(1)}, u32[]{:S(2)}, u32[]{:S(2)}) collective-permute-start(bf16[8,48,256]{2,1,0:T(8,128)(2,1)S(1)} %get-tuple-element.31), channel_id=1, source_target_pairs={{0,1},{1,0},{2,3},{3,2},{4,5},{5,4},{6,7},{7,6},{8,9},{9,8},{10,11... | collective-permute-start | bytes 589832 | tf_op jit(solution)/shard_map/ppermute | solution.py:440
  21.5 7.0 %collective-permute-start.2 = (bf16[8,16,256]{2,1,0:T(8,128)(2,1)S(1)}, bf16[8,16,256]{2,1,0:T(8,128)(2,1)S(1)}, u32[]{:S(2)}, u32[]{:S(2)}) collective-permute-start(bf16[8,16,256]{2,1,0:T(8,128)(2,1)S(1)} %slice.12), channel_id=1, source_target_pairs={{0,2},{1,3},{2,0},{3,1},{4,6},{5,7},{6,4},{7,5},{8,10},{9,11},{10,... | collective-permute-start | bytes 196616 | tf_op jit(solution)/shard_map/ppermute | solution.py:440
  28.5 0.6 copy-start.4
  28.5 0.7 %copy-start.1 = (bf16[8,48,256]{2,1,0:T(8,128)(2,1)}, bf16[8,48,256]{2,1,0:T(8,128)(2,1)S(1)}, u32[]{:S(2)}) copy-start(bf16[8,48,256]{2,1,0:T(8,128)(2,1)S(1)} %collective-permute-done.1.cross_piece) | copy-start | bytes 589828
  29.2 0.7 %copy-start.2 = (bf16[8,48,256]{2,1,0:T(8,128)(2,1)}, bf16[8,48,256]{2,1,0:T(8,128)(2,1)S(1)}, u32[]{:S(2)}) copy-start(bf16[8,48,256]{2,1,0:T(8,128)(2,1)S(1)} %collective-permute-done.core_piece) | copy-start | bytes 589828
  35.6 7.5 %collective-permute-start.5 = (f32[8,256]{1,0:T(8,128)}, f32[8,256]{1,0:T(8,128)S(1)}, u32[]{:S(2)}, u32[]{:S(2)}) collective-permute-start(f32[8,256]{1,0:T(8,128)} %get-tuple-element.16.refs_0_), channel_id=1, source_target_pairs={{0,2},{1,3},{2,0},{3,1},{4,6},{5,7},{6,4},{7,5},{8,10},{9,11},{10,... | collective-permute-start | bytes 24584 | tf_op jit(solution)/shard_map/ppermute | solution.py:440
  35.6 7.5 %collective-permute-start.4 = (f32[8,256]{1,0:T(8,128)}, f32[8,256]{1,0:T(8,128)S(1)}, u32[]{:S(2)}, u32[]{:S(2)}) collective-permute-start(f32[8,256]{1,0:T(8,128)} %get-tuple-element.16.refs_0_), channel_id=1, source_target_pairs={{0,3},{1,2},{2,1},{3,0},{4,7},{5,6},{6,5},{7,4},{8,11},{9,10},{10,... | collective-permute-start | bytes 24584 | tf_op jit(solution)/shard_map/ppermute | solution.py:440
  37.0 6.1 %collective-permute-start.3 = (f32[8,256]{1,0:T(8,128)}, f32[8,256]{1,0:T(8,128)S(1)}, u32[]{:S(2)}, u32[]{:S(2)}) collective-permute-start(f32[8,256]{1,0:T(8,128)} %get-tuple-element.16.refs_0_), channel_id=1, source_target_pairs={{0,1},{1,0},{2,3},{3,2},{4,5},{5,4},{6,7},{7,6},{8,9},{9,8},{10,11... | collective-permute-start | bytes 24584 | tf_op jit(solution)/shard_map/ppermute | solution.py:440
  43.0 0.6 copy-start.10
  43.1 0.6 copy-start.11
  43.1 0.6 copy-start.12
  53.5 10.3 %all-to-all-start.1 = ((f32[8,8,128]{2,1,0:T(8,128)}), f32[8,8,128]{2,1,0:T(8,128)S(1)}, u32[]{:S(2)}, u32[]{:S(2)}) async-start(f32[8,8,128]{2,1,0:T(8,128)} %broadcast_in_dim.5), calls=%async_computation.1 | async-start | bytes 65536 | tf_op jit(solution)/shard_map/all_to_all | solution.py:497
  57.1 1.9 %collective-permute-start.6 = (f32[48,256]{1,0:T(8,128)}, f32[48,256]{1,0:T(8,128)S(1)}, u32[]{:S(2)}, u32[]{:S(2)}) collective-permute-start(f32[48,256]{1,0:T(8,128)} %get-tuple-element.25), channel_id=1, source_target_pairs={{0,1},{1,0},{2,3},{3,2},{4,5},{5,4},{6,7},{7,6},{8,9},{9,8},{10,11... | collective-permute-start | bytes 147464 | tf_op jit(solution)/shard_map/ppermute | solution.py:440
  57.1 4.8 %collective-permute-start.7 = (f32[48,256]{1,0:T(8,128)}, f32[48,256]{1,0:T(8,128)S(1)}, u32[]{:S(2)}, u32[]{:S(2)}) collective-permute-start(f32[48,256]{1,0:T(8,128)} %get-tuple-element.26), channel_id=1, source_target_pairs={{0,2},{1,3},{2,0},{3,1},{4,6},{5,7},{6,4},{7,5},{8,10},{9,11},{10,... | collective-permute-start | bytes 147464 | tf_op jit(solution)/shard_map/ppermute | solution.py:440
  57.8 4.3 %collective-permute-start.8 = (f32[48,256]{1,0:T(8,128)}, f32[48,256]{1,0:T(8,128)S(1)}, u32[]{:S(2)}, u32[]{:S(2)}) collective-permute-start(f32[48,256]{1,0:T(8,128)} %get-tuple-element.27), channel_id=1, source_target_pairs={{0,3},{1,2},{2,1},{3,0},{4,7},{5,6},{6,5},{7,4},{8,11},{9,10},{10,... | collective-permute-start | bytes 147464 | tf_op jit(solution)/shard_map/ppermute | solution.py:440
  59.0 4.8 %copy-start.7 = (f32[48,256]{1,0:T(8,128)}, f32[48,256]{1,0:T(8,128)S(1)}, u32[]{:S(2)}) copy-start(f32[48,256]{1,0:T(8,128)S(1)} %collective-permute-done.6.core) | copy-start | bytes 147460
  62.0 1.8 %copy-start.8 = (f32[48,256]{1,0:T(8,128)}, f32[48,256]{1,0:T(8,128)S(1)}, u32[]{:S(2)}) copy-start(f32[48,256]{1,0:T(8,128)S(1)} %collective-permute-done.7.diag) | copy-start | bytes 147460
  62.1 1.8 %copy-start.9 = (f32[48,256]{1,0:T(8,128)}, f32[48,256]{1,0:T(8,128)S(1)}, u32[]{:S(2)}) copy-start(f32[48,256]{1,0:T(8,128)S(1)} %collective-permute-done.8.cross) | copy-start | bytes 147460
  63.8 0.6 copy-start.3

commit v2 on v1

--- a/solution.py
+++ b/solution.py
@@ -15,6 +15,10 @@
 BLOCK = 8
 HALF = 64
 LANES = 128
+LOG2E = math.log2(math.e)
+FAR = 3e38
+ORDERS = ((0, 1, 2, None), (None, 2, 1, 0))
+GRANT = 20 * 1024 * 1024
 
 
 class Sizes:
@@ -56,10 +60,6 @@
     return [pl.BlockSpec(memory_space=pltpu.VMEM)] * count
 
 
-def smem_spec():
-    return pl.BlockSpec(memory_space=pltpu.SMEM)
-
-
 def patch_lanes(sz, shape, dim):
     index = iota(shape, dim)
     block = index >> 6
@@ -78,7 +78,10 @@
     pick = (lane >= head * per) & (lane < head * per + per)
     pick16 = pick.astype(F32).astype(BF16)
     rows_ref[...] = dot(w_in_ref[...].astype(BF16), pick16)
-    bias_row_ref[...] = jnp.sum(jnp.where(pick, bias_ref[...], 0.0), axis=0, keepdims=True)
+    row_rank = lax.axis_index("aa")
+    row = (iota((1, lanes), 1) // BLOCK) % sz.mid_a + row_rank * sz.rows_a - 1
+    bias = jnp.sum(jnp.where(pick, bias_ref[...], 0.0), axis=0, keepdims=True)
+    bias_row_ref[...] = jnp.where((row >= 0) & (row < sz.grid_a), bias, 0.0)
     inner = iota((HALF, lanes), 0)
     row_in = over_span(inner, sz.span)
     col_in = inner - row_in * sz.span
@@ -87,7 +90,10 @@
     col_out = lane % BLOCK
     step_row = row_in - row_out
     step_col = col_in - col_out
-    usable = inner < sz.halo_a * sz.span
+    from_row = row_in + row_rank * sz.rows_a - 2
+    to_row = row_out + row_rank * sz.rows_a - 1
+    usable = (inner < sz.halo_a * sz.span) & (from_row >= 0) & (from_row < sz.grid_a)
+    usable = usable & (to_row >= 0) & (to_row < sz.grid_a)
     zeros = jnp.zeros((HALF, lanes), F32)
     for three in range(3):
         for four in range(3):
@@ -97,10 +103,12 @@
                     tap = ((one * 3 + two) * 3 + three) * 3 + four
                     match = usable & (step_row == one) & (step_col == two)
                     total = jnp.where(match, rows_ref[tap : tap + 1, :], total)
-            start = three * 4 * HALF + four * HALF
-            t_in_ref[start : start + HALF, :] = total.astype(BF16)
-        start = three * 4 * HALF + 3 * HALF
-        t_in_ref[start : start + HALF, :] = zeros.astype(BF16)
+            for side in range(2):
+                start = ((side * 3 + three) * 4 + ORDERS[side].index(four)) * HALF
+                t_in_ref[start : start + HALF, :] = total.astype(BF16)
+        for side in range(2):
+            start = ((side * 3 + three) * 4 + ORDERS[side].index(None)) * HALF
+            t_in_ref[start : start + HALF, :] = zeros.astype(BF16)
 
     out_lanes = 4 * HALF
     unit = sz.rows_a * BLOCK
@@ -138,7 +146,7 @@
     w_in = jnp.transpose(conv_in, (1, 2, 3, 4, 0)).reshape(81, hidden)
     w_out = jnp.transpose(conv_out, (2, 3, 0, 1, 4)).reshape(9 * hidden, 9)
     w_out = jnp.pad(w_out, ((0, 0), (0, 7)))
-    rows_in = 3 * 4 * HALF
+    rows_in = 2 * 3 * 4 * HALF
     rows_out = 3 * sz.blocks * sz.lanes_mid
     return pl.pallas_call(
         functools.partial(taps_kernel, sz),
@@ -153,65 +161,52 @@
             pltpu.VMEM((81, sz.lanes_mid), F32),
             pltpu.VMEM((sz.mid_a * 9 * hidden, 4 * HALF), F32),
         ],
+        compiler_params=pltpu.CompilerParams(vmem_limit_bytes=GRANT),
         name="taps",
     )(w_in, w_out, bias_in.reshape(hidden, 1))
 
 
-def scores_body(sz, rank_ref, norm_rows, patch_rows, tile_b, u_ref, part_ref, own_ref):
-    channels = sz.channels
+def spread_kernel(a_ref, b_ref, out_ref):
+    cells = a_ref.shape[0]
+    for at in range(out_ref.shape[0]):
+        out_ref[at, 0:cells, :] = a_ref[...]
+        out_ref[at, cells:, :] = b_ref[...]
+
+
+def scores_body(sz, norm_rows, patch_rows, tile_b, u_ref, part_ref, near_ref, all_ref):
     source = patch_rows.shape[0]
     row, col, inside = patch_lanes(sz, (sz.lanes_in, source), 0)
     at = iota((sz.lanes_in, source), 1)
     wanted = (col >> 3) * (sz.halo_a * BLOCK) + row * BLOCK + (col & (BLOCK - 1))
     pick = (inside & (at == wanted)).astype(F32).astype(BF16)
     patches = dot(pick, patch_rows[...]).astype(BF16)
-    chunk = 512
-    chunks = norm_rows.shape[0] // chunk
-
-    def per_row(index, carry):
-        rows = tile_b[pl.ds(pl.multiple_of(index * LANES, LANES), LANES), :]
-
-        def per_chunk(step, state):
-            best, mass = state
-            block = norm_rows[pl.ds(pl.multiple_of(step * chunk, chunk), chunk), :]
-            scores = dot(rows, block, NT) * sz.scale
-            fresh = jnp.maximum(best, jnp.max(scores, axis=1, keepdims=True))
-            mass = mass * jnp.exp(best - fresh) + jnp.sum(jnp.exp(scores - fresh), axis=1, keepdims=True)
-            return fresh, mass
-
-        if chunks == 1:
-            scores = dot(rows, norm_rows[...], NT) * sz.scale
-            best = jnp.max(scores, axis=1, keepdims=True)
-            mass = jnp.sum(jnp.exp(scores - best), axis=1, keepdims=True)
-        else:
-            start = jnp.full((LANES, 1), -jnp.inf, F32), jnp.zeros((LANES, 1), F32)
-            best, mass = lax.fori_loop(0, chunks, per_chunk, start)
-        norm_a = best + jnp.log(mass)
-        near = dot(rows, patches, NT) * sz.scale
-        place = pl.ds(pl.multiple_of(index * LANES, LANES), LANES)
-        own_ref[place, :] = near
-        u_ref[place, :] = 2.0 * near - norm_a + sz.offset
-        return carry
-
-    lax.fori_loop(0, sz.halo_b, per_row, 0)
-    own = own_ref[2 * LANES : (2 + sz.rows_b) * LANES, :]
-    best = jnp.max(own, axis=0, keepdims=True)
-    mass = jnp.sum(jnp.exp(own - best), axis=0, keepdims=True)
+    near_ref[...] = dot(tile_b[...], patches, NT)
+    all_ref[...] = dot(tile_b[...], norm_rows[...], NT)
+    steep = sz.scale * LOG2E
+    for index in range(sz.halo_b):
+        place = slice(index * LANES, (index + 1) * LANES)
+        best = jnp.max(all_ref[place, :], axis=1, keepdims=True)
+        mass = jnp.sum(jnp.exp2((all_ref[place, :] - best) * steep), axis=1, keepdims=True)
+        shift = sz.offset - (best * sz.scale + jnp.log(mass))
+        u_ref[place, :] = near_ref[place, :] * (2.0 * sz.scale) + shift
+    own = slice(2 * LANES, (2 + sz.rows_b) * LANES)
+    best = jnp.max(near_ref[own, :], axis=0, keepdims=True)
+    mass = jnp.sum(jnp.exp2((near_ref[own, :] - best) * steep), axis=0, keepdims=True)
     part_ref[...] = jnp.concatenate(
-        [best, mass, jnp.zeros((6, sz.lanes_in), F32)], axis=0
-    )
-
-
-def scores_kernel_direct(sz, rank_ref, norm_rows, patch_rows, tile_b, u_ref, part_ref, own_ref):
-    scores_body(sz, rank_ref, norm_rows, patch_rows, tile_b, u_ref, part_ref, own_ref)
+        [best * sz.scale, mass, jnp.zeros((6, sz.lanes_in), F32)], axis=0
+    )
+
+
+def scores_kernel_direct(sz, norm_rows, patch_rows, tile_b, u_ref, part_ref, near_ref, all_ref):
+    scores_body(sz, norm_rows, patch_rows, tile_b, u_ref, part_ref, near_ref, all_ref)
 
 
 def scores_kernel_pieces(
-    sz, count, rank_ref, own_piece, core_piece, cross_piece, diag_piece,
+    sz, count, own_piece, core_piece, cross_piece, diag_piece,
     u_ref, part_ref, own_a_ref, own_b_ref,
-    norm_rows, patch_rows, tile_b, near_ref,
+    norm_rows, patch_rows, tile_b, near_ref, all_ref,
 ):
-    row_rank, col_rank = rank_ref[0], rank_ref[1]
+    row_rank, col_rank = lax.axis_index("aa"), lax.axis_index("ba")
     cells = sz.rows_a * BLOCK
     cols = sz.width_b // count
     pieces = ((own_piece, 0), (core_piece, 1), (diag_piece, 2), (cross_piece, 3))
@@ -237,20 +232,17 @@
         for row in range(2):
             rows = piece[:, cells + row * cols : cells + (row + 1) * cols, :].reshape(width, sz.channels)
             tile_b[pl.ds(pl.multiple_of(base + row * width, width), width), :] = rows
-    scores_body(sz, rank_ref, norm_rows, patch_rows, tile_b, u_ref, part_ref, near_ref)
+    scores_body(sz, norm_rows, patch_rows, tile_b, u_ref, part_ref, near_ref, all_ref)
 
 
 def softplus(values):
-    return jnp.maximum(values, 0.0) + jnp.log1p(jnp.exp(-jnp.abs(values)))
-
-
-def refine_kernel(sz, parts, split, rank_ref, u_ref, *refs):
+    return jnp.maximum(values, 0.0) + jnp.log(1.0 + jnp.exp(-jnp.abs(values)))
+
+
+def refine_kernel(sz, parts, u_ref, *refs):
     part_refs = refs[:parts]
-    t_in, t_out, bias_row, own_a, own_b = refs[parts : parts + 5]
-    outs = refs[parts + 5 : -4]
-    refined_ref, sums_a_ref = outs[0], outs[1]
-    x_ref, mid_ref, share_ref, stat_ref = refs[-4:]
-    row_rank, col_rank = rank_ref[0], rank_ref[1]
+    t_in, t_out, bias_row, own_a, own_b, refined_ref, sums_ref, pad_ref, x_ref, mid_ref = refs[parts:]
+    col_rank = lax.axis_index("ba")
     last = sz.grid_b // sz.rows_b - 1
     tops, masses = [], []
     for ref in part_refs:
@@ -262,72 +254,48 @@
     norm_b = top + jnp.log(mass)
 
     row, _, inside = patch_lanes(sz, (1, sz.lanes_in), 1)
-    row = row + row_rank * sz.rows_a - 2
-    inside = inside & (row >= 0) & (row < sz.grid_a)
-    lane = iota((LANES, LANES), 1)
+    norm_b = jnp.where(inside, norm_b, FAR)
+    low = iota((LANES, LANES), 1) < HALF
     line = iota((LANES, LANES), 0)
-    low = lane < HALF
-    low_down = low & (line > 0)
-    low_up = low & (line < LANES - 1)
-
-    def place_matched(index, carry):
-        place = pl.ds(pl.multiple_of(index * LANES, LANES), LANES)
-        matched = softplus(u_ref[place, :] - norm_b)
-        matched = jnp.where(inside, matched, 0.0)
-        for pair in range(sz.blocks // 2):
-            here = matched[:, pair * LANES : (pair + 1) * LANES]
-            turned = pltpu.roll(here, HALF, 1)
-            for side, (one, two) in enumerate(((here, turned), (turned, here))):
-                block = pair * 2 + side
-                first = jnp.where(low, jnp.where(low_down, pltpu.roll(one, 1, 0), 0.0), two)
-                second = jnp.where(low_up, pltpu.roll(one, LANES - 1, 0), 0.0)
-                x_ref[block, place, 0:LANES] = first.astype(BF16)
-                x_ref[block, place, LANES : 2 * LANES] = second.astype(BF16)
-        return carry
-
-    lax.fori_loop(0, sz.halo_b, place_matched, 0)
-    edge = 2 * LANES
-    far = (2 + sz.rows_b) * LANES
-
-    @pl.when(col_rank == 0)
-    def _():
-        x_ref[:, 0:edge, :] = jnp.zeros((sz.blocks, edge, 2 * LANES), BF16)
-
-    @pl.when(col_rank == last)
-    def _():
-        x_ref[:, far : far + edge, :] = jnp.zeros((sz.blocks, edge, 2 * LANES), BF16)
-
     rows_mid = sz.mid_b * LANES
-    lane = iota((1, sz.lanes_mid), 1)
-    row = (lane // BLOCK) % sz.mid_a + row_rank * sz.rows_a - 1
-    inside_mid = (row >= 0) & (row < sz.grid_a)
+    depth = 3 * 4 * HALF
     bias = bias_row[...]
-    for block in range(sz.blocks):
-        total = bias
-        for three in range(3):
-            total = total + dot(
-                x_ref[block, three * LANES : three * LANES + rows_mid, :],
-                t_in[three * 4 * HALF : (three + 1) * 4 * HALF, :],
+    for pair in range(sz.blocks // 2):
+        lanes = slice(pair * LANES, (pair + 1) * LANES)
+        for index in range(sz.halo_b):
+            norm = norm_b[:, lanes]
+            if index < 2:
+                norm = jnp.where(col_rank == 0, FAR, norm)
+            if index >= sz.halo_b - 2:
+                norm = jnp.where(col_rank == last, FAR, norm)
+            place = slice(index * LANES, (index + 1) * LANES)
+            matched = softplus(u_ref[place, lanes] - norm)
+            pad_ref[pair, index, 0:8, :] = jnp.zeros((8, LANES), F32)
+            pad_ref[pair, index, 8 + LANES :, :] = jnp.zeros((8, LANES), F32)
+            pad_ref[pair, index, 8 : 8 + LANES, :] = matched
+            turned = pltpu.roll(matched, HALF, 1)
+            down = pad_ref[pair, index, 7 : 7 + LANES, :]
+            x_ref[pair, place, 0:LANES] = jnp.where(low, down, turned).astype(BF16)
+            x_ref[pair, place, LANES : 2 * LANES] = pad_ref[pair, index, 9 : 9 + LANES, :].astype(BF16)
+            x_ref[pair, place, 2 * LANES :] = jnp.where(low, turned, down).astype(BF16)
+        for side in range(2):
+            lanes = slice(side * LANES, (side + 2) * LANES)
+            stacked = jnp.concatenate(
+                [x_ref[pair, three * LANES : three * LANES + rows_mid, lanes] for three in range(3)], axis=1
             )
-        hidden = jnp.where(inside_mid, jnp.maximum(total, 0.0), 0.0)
-        mid_ref[:, block * sz.lanes_mid : (block + 1) * sz.lanes_mid] = hidden.astype(BF16)
-    wide = sz.blocks * sz.lanes_mid
-
-    @pl.when(col_rank == 0)
-    def _():
-        mid_ref[0:LANES, :] = jnp.zeros((LANES, wide), BF16)
-
-    @pl.when(col_rank == last)
-    def _():
-        mid_ref[rows_mid - LANES : rows_mid, :] = jnp.zeros((LANES, wide), BF16)
-
-    spread = 0.0
-    for three in range(3):
-        spread = spread + dot(
-            mid_ref[three * LANES : three * LANES + sz.cells_b, :],
-            t_out[three * wide : (three + 1) * wide, :],
-        )
-    best_b = None
+            total = dot(stacked, t_in[side * depth : (side + 1) * depth, :]) + bias
+            hidden = jnp.maximum(total, 0.0).astype(BF16)
+            start = (pair * 2 + side) * sz.lanes_mid
+            lanes = slice(start, start + sz.lanes_mid)
+            head, tail = hidden[0:LANES], hidden[rows_mid - LANES :]
+            mid_ref[0:LANES, lanes] = jnp.where(col_rank == 0, jnp.zeros_like(head), head)
+            mid_ref[LANES : rows_mid - LANES, lanes] = hidden[LANES : rows_mid - LANES]
+            mid_ref[rows_mid - LANES :, lanes] = jnp.where(col_rank == last, jnp.zeros_like(tail), tail)
+    stacked = jnp.concatenate(
+        [mid_ref[three * LANES : three * LANES + sz.cells_b, :] for three in range(3)], axis=1
+    )
+    spread = dot(stacked, t_out[...])
+    tops, masses = [], []
     for row in range(sz.rows_b):
         left = spread[row * LANES : (row + 1) * LANES, 0:LANES]
         right = spread[row * LANES : (row + 1) * LANES, LANES : 2 * LANES]
@@ -340,13 +308,15 @@
         scores = dot(own_a[...], own_b[row * LANES : (row + 1) * LANES, :], NT) * sz.scale
         refined = scores + filtered
         refined_ref[:, row * LANES : (row + 1) * LANES] = refined
-        top = jnp.max(refined, axis=0, keepdims=True)
-        sums_a_ref[row : row + 1, :] = top
-        sums_a_ref[sz.rows_b + row : sz.rows_b + row + 1, :] = jnp.sum(
-            jnp.exp(refined - top), axis=0, keepdims=True
-        )
-        best = jnp.max(refined, axis=1, keepdims=True)
-        best_b = best if best_b is None else jnp.maximum(best_b, best)
+        tops.append(jnp.max(refined, axis=0, keepdims=True))
+        masses.append(jnp.sum(jnp.exp(refined - tops[-1]), axis=0, keepdims=True))
+    sums = jnp.concatenate(tops + masses, axis=0)
+    for at in range(sums_ref.shape[0]):
+        sums_ref[at] = sums
+
+
+def share_kernel(sz, split, refined_ref, own_b, *refs):
+    best_b = jnp.max(refined_ref[...], axis=1, keepdims=True)
     weights = jnp.exp(refined_ref[...] - best_b)
     total_b = jnp.sum(weights, axis=1, keepdims=True)
     high = weights.astype(BF16)
@@ -355,21 +325,21 @@
     lane = iota((HALF, LANES), 1)
     stats = jnp.where(lane < HALF, best_b, total_b)
     if not split:
-        outs[2][...] = share
-        outs[3][...] = stats
+        refs[0][...] = share
+        refs[1][...] = stats
         return
+    share_ref = refs[4]
     share_ref[...] = share
     cells = sz.rows_a * BLOCK
     for flip in range(4):
-        out = outs[2 + flip]
-        start = pl.multiple_of((col_rank ^ flip) * cells, cells)
-        out[0:cells, :] = share_ref[pl.ds(start, cells), :]
-        out[cells:, 0:LANES] = stats[0 : HALF // 2, :]
-        out[cells:, LANES:] = stats[HALF // 2 :, :]
-
-
-def finish_kernel(sz, count, rank_ref, refined_ref, sums_ref, own, core, diag, cross, out_ref, warped_ref, stat_ref):
-    col_rank = rank_ref[1]
+        start = pl.multiple_of((lax.axis_index("ba") ^ flip) * cells, cells)
+        refs[flip][0:cells, :] = share_ref[pl.ds(start, cells), :]
+        refs[flip][cells:, 0:LANES] = stats[0 : HALF // 2, :]
+        refs[flip][cells:, LANES:] = stats[HALF // 2 :, :]
+
+
+def finish_kernel(sz, count, refined_ref, sums_ref, own, core, diag, cross, out_ref, warped_ref, stat_ref):
+    col_rank = lax.axis_index("ba")
     cells = sz.rows_a * BLOCK
     lane = iota((HALF, LANES), 1)
     tops, masses = [], []
@@ -412,28 +382,34 @@
     return pl.pallas_call(
         kernel,
         out_shape=outs,
-        in_specs=[smem_spec()] + vmem_specs(len(args) - 1),
+        in_specs=vmem_specs(len(args)),
         out_specs=tuple(vmem_specs(len(outs))),
         scratch_shapes=scratch,
+        compiler_params=pltpu.CompilerParams(vmem_limit_bytes=GRANT),
         name=name,
     )(*args)
 
 
-def refine_call(sz, parts, split, *args):
+def refine_call(sz, parts, copies, *args):
     shape = jax.ShapeDtypeStruct
-    cells = sz.rows_a * BLOCK
-    outs = [shape((HALF, sz.cells_b), F32), shape((8, LANES), F32)]
+    outs = (shape((HALF, sz.cells_b), F32), shape((copies, 8, LANES), F32))
+    scratch = [
+        pltpu.VMEM((sz.blocks // 2, sz.halo_b, LANES + 16, LANES), F32),
+        pltpu.VMEM((sz.blocks // 2, sz.halo_b * LANES, 3 * LANES), BF16),
+        pltpu.VMEM((sz.mid_b * LANES, sz.blocks * sz.lanes_mid), BF16),
+    ]
+    return call(functools.partial(refine_kernel, sz, parts), "refine", outs, scratch, *args)
+
+
+def share_call(sz, split, *args):
+    shape = jax.ShapeDtypeStruct
     if split:
-        outs += [shape((cells + HALF // 2, 2 * LANES), F32)] * 4
+        outs = (shape((sz.rows_a * BLOCK + HALF // 2, 2 * LANES), F32),) * 4
+        scratch = [pltpu.VMEM((HALF, sz.channels), F32)]
     else:
-        outs += [shape((HALF, sz.channels), F32), shape((HALF, LANES), F32)]
-    scratch = [
-        pltpu.VMEM((sz.blocks, sz.halo_b * LANES, 2 * LANES), BF16),
-        pltpu.VMEM((sz.mid_b * LANES, sz.blocks * sz.lanes_mid), BF16),
-        pltpu.VMEM((HALF, sz.channels), F32),
-        pltpu.VMEM((HALF, LANES), F32),
-    ]
-    return call(functools.partial(refine_kernel, sz, parts, split), "refine", tuple(outs), scratch, *args)
+        outs = (shape((HALF, sz.channels), F32), shape((HALF, LANES), F32))
+        scratch = []
+    return call(functools.partial(share_kernel, sz, split), "share", outs, scratch, *args)
 
 
 def swap(value, flip, count):
@@ -454,14 +430,18 @@
     sz = sizes_of(features_a, features_b, conv_in)
     count = lax.axis_size("aa")
     shape = jax.ShapeDtypeStruct
-    row_rank, col_rank = lax.axis_index("aa"), lax.axis_index("ba")
-    rank = jnp.stack([row_rank, col_rank]).astype(jnp.int32)
+    col_rank = lax.axis_index("ba")
     cells = sz.rows_a * BLOCK
     cols = features_b.shape[1]
-    mine = jnp.concatenate(
-        [features_a.reshape(cells, sz.channels), features_b.reshape(-1, sz.channels)], axis=0
-    )
-    spread = jnp.broadcast_to(mine[None], (count,) + mine.shape)
+    fine_a = features_a.reshape(cells, sz.channels)
+    fine_b = features_b.reshape(-1, sz.channels)
+    (spread,) = call(
+        spread_kernel,
+        "spread",
+        (shape((count, cells + fine_b.shape[0], sz.channels), BF16),),
+        [],
+        fine_a, fine_b,
+    )
     own = lax.all_to_all(spread, "aa", 0, 0, tiled=True)
     rows_here = own[:, 0:cells]
     first = own[:, cells : cells + 2 * cols]
@@ -485,16 +465,17 @@
             pltpu.VMEM((sz.halo_a * sz.width_a, sz.channels), BF16),
             pltpu.VMEM((sz.halo_b * LANES, sz.channels), BF16),
             pltpu.VMEM((sz.halo_b * LANES, sz.lanes_in), F32),
+            pltpu.VMEM((sz.halo_b * LANES, sz.grid_a * sz.width_a), F32),
         ],
-        rank, own, core, cross, diag,
+        own, core, cross, diag,
     )
     others = [swap(part, flip, 4) for flip in (1, 3, 2)]
-    refined, sums_a, *bundles = refine_call(
-        sz, 4, True, rank, u, part, *others, t_in, t_out, bias_row, own_a, own_b
-    )
+    refined, sums = refine_call(
+        sz, 4, count, u, part, *others, t_in, t_out, bias_row, own_a, own_b
+    )
+    sums = lax.all_to_all(sums, "aa", 0, 0, tiled=True).reshape(count * 8, LANES)
+    bundles = share_call(sz, True, refined, own_b)
     moved = [swap(bundles[flip], flip, 4) for flip in (1, 3, 2)]
-    sums = jnp.broadcast_to(sums_a[None], (count,) + sums_a.shape)
-    sums = lax.all_to_all(sums, "aa", 0, 0, tiled=True).reshape(count * 8, LANES)
     return call(
         functools.partial(finish_kernel, sz, count),
         "finish",
@@ -503,7 +484,7 @@
             shape((sz.rows_a, BLOCK, sz.channels), F32),
         ),
         [pltpu.VMEM((5, HALF, LANES), F32)],
-        rank, refined, sums, bundles[0], moved[0], moved[2], moved[1],
+        refined, sums, bundles[0], moved[0], moved[2], moved[1],
     )
 
 
@@ -511,8 +492,7 @@
     sz = sizes_of(features_a, features_b, conv_in)
     count_b = lax.axis_size("ba")
     shape = jax.ShapeDtypeStruct
-    row_rank, col_rank = lax.axis_index("aa"), lax.axis_index("ba")
-    rank = jnp.stack([row_rank, col_rank]).astype(jnp.int32)
+    row_rank = lax.axis_index("aa")
     channels = sz.channels
     rows_a = lax.all_gather(features_a, "ba", axis=1, tiled=True)
     all_a = lax.all_gather(rows_a, "aa", axis=0, tiled=True)
@@ -534,13 +514,19 @@
         functools.partial(scores_kernel_direct, sz),
         "scores",
         (shape((sz.halo_b * LANES, sz.lanes_in), F32), shape((8, sz.lanes_in), F32)),
-        [pltpu.VMEM((sz.halo_b * LANES, sz.lanes_in), F32)],
-        rank, all_a.reshape(-1, channels), blocked(around), tile_b,
+        [
+            pltpu.VMEM((sz.halo_b * LANES, sz.lanes_in), F32),
+            pltpu.VMEM((sz.halo_b * LANES, sz.grid_a * sz.width_a), F32),
+        ],
+        all_a.reshape(-1, channels), blocked(around), tile_b,
     )
     parts = lax.all_gather(part, "ba", axis=0, tiled=True)
-    refined, sums_a, share, stats = refine_call(
-        sz, 1, False, rank, u, parts, t_in, t_out, bias_row, blocked(rows_a), rows_b.reshape(-1, channels)
-    )
+    whole_b = rows_b.reshape(-1, channels)
+    refined, sums_a = refine_call(
+        sz, 1, 1, u, parts, t_in, t_out, bias_row, blocked(rows_a), whole_b
+    )
+    sums_a = sums_a[0]
+    share, stats = share_call(sz, False, refined, whole_b)
     top, mass = stats[:, 0], stats[:, HALF]
     best = lax.pmax(top, "ba")
     norm_b = best + jnp.log(lax.psum(mass * jnp.exp(top - best), "ba"))

time: 66.8 us -> 50.3 us (0.75)
  Pallas kernels: 19.3 us -> 8.8 us
  local copies, waits for them, and re-layouts: 6.73 us -> 1.78 us
  other arithmetic: 1.41 us -> 0.05 us
    pallas_call x3 -> x5, Pallas kernels: 16.1 us -> 7.53 us  [call(): pl.pallas_call(kernel, out_shape=outs, in_specs=vmem_specs(len(args)), ou...]
    broadcast_in_dim x2 -> x0, local copies, waits for them, and re-layouts: 2.02 us -> none  [the longest x1 1.28 us: local_four(): sums = jnp.broadcast_to(sums_a[None], (count,) + sums_a.shape)]
    pallas_call x1, Pallas kernels: 3.18 us -> 1.27 us  [build_taps(): pl.pallas_call(functools.partial(taps_kernel, sz), out_shape=(jax.ShapeDt...]
    unnamed x28 -> x10, local copies, waits for them, and re-layouts: 2.57 us -> 1.46 us
    ppermute x9, waiting for transfers between devices: 8.96 us -> 9.72 us  [swap(): return lax.ppermute(value, 'ba', [(at, at ^ flip) for at in range(count)])]
    concatenate x1 -> x0, other arithmetic: 0.76 us -> none  [local_four(): jnp.concatenate([features_a.reshape(cells, sz.channels), features_b.resha...]
  transfers between devices with their start and end apart: 11 -> 11, of which waited for: 5 -> 5; matrix products, arithmetic and copies ran while one was open for 4% -> 1% of each run, Pallas kernels for 5% -> 3%
where the time goes in v2:
time: 50.3 us; the launch traced here: 49.9 us
  waiting for transfers between devices  21.3 us (42%)
  starting transfers between devices  17.2 us (34%)
  Pallas kernels  8.8 us (17%)
  local copies, waits for them, and re-layouts  1.78 us (4%)
  between operations  0.76 us (2%)
    all_to_all x1, waiting for transfers between devices, local_four(): own = lax.all_to_all(spread, 'aa', 0, 0, tiled=True)  10.3 us
    ppermute x9, waiting for transfers between devices, swap(): return lax.ppermute(value, 'ba', [(at, at ^ flip) for at in range(count)])  9.72 us
    pallas_call x5, Pallas kernels, call(): pl.pallas_call(kernel, out_shape=outs, in_specs=vmem_specs(len(args)), ou...  7.53 us
    all_to_all x1, starting transfers between devices, local_four(): own = lax.all_to_all(spread, 'aa', 0, 0, tiled=True)  7.28 us
    ppermute x9, starting transfers between devices, swap(): return lax.ppermute(value, 'ba', [(at, at ^ flip) for at in range(count)])  6.32 us
    all_to_all x1, starting transfers between devices, local_four(): lax.all_to_all(sums, 'aa', 0, 0, tiled=True).reshape(count * 8, LANES)  3.62 us
    unnamed x10, local copies, waits for them, and re-layouts  1.46 us
    pallas_call x1, Pallas kernels, build_taps(): pl.pallas_call(functools.partial(taps_kernel, sz), out_shape=(jax.ShapeDt...  1.27 us
  transfers between devices with their start and end apart: 11, of which 5 were waited for; matrix products, arithmetic and copies ran while one was open for 1% of the time, Pallas kernels for 3%

profile of v2, /device:TPU:0, one launch (start us, length us, event | category | flops | bytes accessed | tf_op | source)
XLA Modules:
  0.0 49.9 jit_solution(5126414620001251943)
XLA Ops:
  0.6 0.0 copy-start
  0.6 0.7 %copy-done = bf16[4,16,256]{2,1,0:T(8,128)(2,1)S(1)} copy-done((bf16[4,16,256]{2,1,0:T(8,128)(2,1)S(1)}, bf16[4,16,256]{2,1,0:T(8,128)(2,1)}, u32[]{:S(2)}) %copy-start) | copy-done | bytes 32792
  1.4 0.0 copy-start.1
  1.4 0.7 %copy-done.1 = bf16[2,8,256]{2,1,0:T(8,128)(2,1)S(1)} copy-done((bf16[2,8,256]{2,1,0:T(8,128)(2,1)S(1)}, bf16[2,8,256]{2,1,0:T(8,128)(2,1)}, u32[]{:S(2)}) %copy-start.1) | copy-done | bytes 8216
  2.1 0.0 copy-start.4
  2.1 0.0 copy-start.2
  2.1 0.0 copy-start.3
  2.1 0.7 %spread.1 = bf16[8,80,256]{2,1,0:T(8,128)(2,1)} custom-call(bf16[16,256]{1,0:T(8,128)(2,1)S(1)} %bitcast.10, bf16[64,256]{1,0:T(8,128)(2,1)S(1)} %bitcast.9), custom_call_target="tpu_custom_call" | custom-call | tf_op jit(solution)/shard_map/spread/pallas_call | solution.py:382
  2.8 7.3 %all-to-all-start = ((bf16[8,80,256]{2,1,0:T(8,128)(2,1)}), bf16[8,80,256]{2,1,0:T(8,128)(2,1)S(1)}, u32[]{:S(2)}, u32[]{:S(2)}) async-start(bf16[8,80,256]{2,1,0:T(8,128)(2,1)} %spread.1), calls=%async_computation | async-start | bytes 655360 | tf_op jit(solution)/shard_map/all_to_all | solution.py:445
  10.1 10.3 %all-to-all-done.own_piece = bf16[8,80,256]{2,1,0:T(8,128)(2,1)S(1)} async-done(((bf16[8,80,256]{2,1,0:T(8,128)(2,1)}), bf16[8,80,256]{2,1,0:T(8,128)(2,1)S(1)}, u32[]{:S(2)}, u32[]{:S(2)}) %all-to-all-start) | async-done | bytes 327712 | tf_op jit(solution)/shard_map/all_to_all | solution.py:445
  20.5 0.1 collective-permute-start.1
  20.6 1.6 %collective-permute-start = (bf16[8,48,256]{2,1,0:T(8,128)(2,1)S(1)}, bf16[8,48,256]{2,1,0:T(8,128)(2,1)S(1)}, u32[]{:S(2)}, u32[]{:S(2)}) collective-permute-start(bf16[8,48,256]{2,1,0:T(8,128)(2,1)S(1)} %get-tuple-element.31), channel_id=1, source_target_pairs={{0,1},{1,0},{2,3},{3,2},{4,5},{5,4},{6,7},{7,6},{8,9},{9,8},{10,11... | collective-permute-start | bytes 589832 | tf_op jit(solution)/shard_map/ppermute | solution.py:416
  22.2 0.5 %collective-permute-start.2 = (bf16[8,16,256]{2,1,0:T(8,128)(2,1)S(1)}, bf16[8,16,256]{2,1,0:T(8,128)(2,1)S(1)}, u32[]{:S(2)}, u32[]{:S(2)}) collective-permute-start(bf16[8,16,256]{2,1,0:T(8,128)(2,1)S(1)} %slice.12), channel_id=1, source_target_pairs={{0,2},{1,3},{2,0},{3,1},{4,6},{5,7},{6,4},{7,5},{8,10},{9,11},{10,... | collective-permute-start | bytes 196616 | tf_op jit(solution)/shard_map/ppermute | solution.py:416
  22.7 6.5 %collective-permute-done.2.diag_piece = bf16[8,16,256]{2,1,0:T(8,128)(2,1)S(1)} collective-permute-done((bf16[8,16,256]{2,1,0:T(8,128)(2,1)S(1)}, bf16[8,16,256]{2,1,0:T(8,128)(2,1)S(1)}, u32[]{:S(2)}, u32[]{:S(2)}) %collective-permute-start.2) | collective-permute-done | bytes 65568 | tf_op jit(solution)/shard_map/ppermute | solution.py:416
  29.2 0.0 collective-permute-done.1.cross_piece
  29.2 0.0 collective-permute-done.core_piece
  29.2 1.2 %scores.1 = (f32[1024,256]{1,0:T(8,128)S(1)}, f32[8,256]{1,0:T(8,128)S(1)}, bf16[64,256]{1,0:T(8,128)(2,1)S(1)}, bf16[512,256]{1,0:T(8,128)(2,1)S(1)}) custom-call(bf16[8,80,256]{2,1,0:T(8,128)(2,1)S(1)} %all-to-all-done.own_piece, bf16[8,48,256]{2,1,0:T(8,128)(2,1)S(1)} %collective-permute-done.core_piece, ...), custom_call_target="tpu_custom_call" | custom-call | tf_op jit(solution)/shard_map/scores/pallas_call | solution.py:382
  30.3 0.1 collective-permute-start.5
  30.4 1.4 %collective-permute-start.4 = (f32[8,256]{1,0:T(8,128)S(1)}, f32[8,256]{1,0:T(8,128)S(1)}, u32[]{:S(2)}, u32[]{:S(2)}) collective-permute-start(f32[8,256]{1,0:T(8,128)S(1)} %get-tuple-element.16.refs_0_), channel_id=1, source_target_pairs={{0,3},{1,2},{2,1},{3,0},{4,7},{5,6},{6,5},{7,4},{8,11},{9,10},{10,... | collective-permute-start | bytes 24584 | tf_op jit(solution)/shard_map/ppermute | solution.py:416
  31.8 0.8 %collective-permute-start.3 = (f32[8,256]{1,0:T(8,128)S(1)}, f32[8,256]{1,0:T(8,128)S(1)}, u32[]{:S(2)}, u32[]{:S(2)}) collective-permute-start(f32[8,256]{1,0:T(8,128)S(1)} %get-tuple-element.16.refs_0_), channel_id=1, source_target_pairs={{0,1},{1,0},{2,3},{3,2},{4,5},{5,4},{6,7},{7,6},{8,9},{9,8},{10,11... | collective-permute-start | bytes 24584 | tf_op jit(solution)/shard_map/ppermute | solution.py:416
  32.5 0.0 copy-done.4
  32.5 0.1 copy.11.bias_ref
  32.6 0.0 copy-done.2
  32.6 0.0 copy-done.3
  32.7 0.1 reshape.25
  32.8 0.1 copy.10
  32.9 1.3 %taps.1 = (bf16[1536,256]{1,0:T(8,128)(2,1)S(1)}, bf16[3072,256]{1,0:T(8,128)(2,1)S(1)}, f32[1,256]{1,0:T(1,128)S(1)}) custom-call(f32[81,8]{1,0:T(8,128)S(1)} %reshape.24.w_in_ref, f32[72,16]{1,0:T(8,128)S(1)} %pad.4.w_out_ref, f32[8,1]{1,0:T(8,128)S(1)} %copy.11.bias_ref), custom_call_target="tpu_custom_call" | custom-call | tf_op jit(solution)/shard_map/taps/pallas_call | solution.py:151
  34.2 0.0 collective-permute-done.5.refs_3_
  34.2 0.0 collective-permute-done.4.refs_2_
  34.2 0.0 collective-permute-done.3.refs_1_
  34.2 4.5 %refine.1 = (f32[64,512]{1,0:T(8,128)S(1)}, f32[8,8,128]{2,1,0:T(8,128)}) custom-call(f32[1024,256]{1,0:T(8,128)S(1)} %get-tuple-element.15.u_ref, f32[8,256]{1,0:T(8,128)S(1)} %get-tuple-element.16.refs_0_, f32[8,256]{1,0:T(8,128)S(1)} %collective-permute-done.3.refs_1_, f32[8,256]{1,0:T(8,128)S(1)} %collective-permute-done.4.refs_2_, ...), custom_call_target="tpu_custom_call" | custom-call | tf_op jit(solution)/shard_map/refine/pallas_call | solution.py:382
  38.7 3.6 %all-to-all-start.1 = ((f32[8,8,128]{2,1,0:T(8,128)}), f32[8,8,128]{2,1,0:T(8,128)S(1)}, u32[]{:S(2)}, u32[]{:S(2)}) async-start(f32[8,8,128]{2,1,0:T(8,128)} %get-tuple-element.23), calls=%async_computation.1 | async-start | bytes 65536 | tf_op jit(solution)/shard_map/all_to_all | solution.py:476
  42.3 0.3 share.1
  42.6 0.1 collective-permute-start.6
  42.6 1.4 %collective-permute-start.7 = (f32[48,256]{1,0:T(8,128)S(1)}, f32[48,256]{1,0:T(8,128)S(1)}, u32[]{:S(2)}, u32[]{:S(2)}) collective-permute-start(f32[48,256]{1,0:T(8,128)S(1)} %get-tuple-element.26), channel_id=1, source_target_pairs={{0,2},{1,3},{2,0},{3,1},{4,6},{5,7},{6,4},{7,5},{8,10},{9,11},{10,... | collective-permute-start | bytes 147464 | tf_op jit(solution)/shard_map/ppermute | solution.py:416
  44.0 0.5 collective-permute-start.8
  44.5 0.0 collective-permute-done.6.core
  44.5 2.3 %collective-permute-done.7.diag = f32[48,256]{1,0:T(8,128)S(1)} collective-permute-done((f32[48,256]{1,0:T(8,128)S(1)}, f32[48,256]{1,0:T(8,128)S(1)}, u32[]{:S(2)}, u32[]{:S(2)}) %collective-permute-start.7) | collective-permute-done | bytes 49184 | tf_op jit(solution)/shard_map/ppermute | solution.py:416
  46.8 0.9 %collective-permute-done.8.cross = f32[48,256]{1,0:T(8,128)S(1)} collective-permute-done((f32[48,256]{1,0:T(8,128)S(1)}, f32[48,256]{1,0:T(8,128)S(1)}, u32[]{:S(2)}, u32[]{:S(2)}) %collective-permute-start.8) | collective-permute-done | bytes 49184 | tf_op jit(solution)/shard_map/ppermute | solution.py:416
  47.7 1.2 %all-to-all-done.1 = f32[8,8,128]{2,1,0:T(8,128)S(1)} async-done(((f32[8,8,128]{2,1,0:T(8,128)}), f32[8,8,128]{2,1,0:T(8,128)S(1)}, u32[]{:S(2)}, u32[]{:S(2)}) %all-to-all-start.1) | async-done | bytes 32800 | tf_op jit(solution)/shard_map/all_to_all | solution.py:476
  49.0 0.9 %finish.1 = (f32[2,32,4,128]{3,2,1,0:T(4,128)}, f32[2,8,256]{2,1,0:T(8,128)}) custom-call(f32[64,512]{1,0:T(8,128)S(1)} %get-tuple-element.22.refined_ref, f32[64,128]{1,0:T(8,128)S(1)} %bitcast.8, f32[48,256]{1,0:T(8,128)S(1)} %get-tuple-element.24.own, f32[48,256]{1,0:T(8,128)S(1)} %collective-permute-done.6.core, ...), custom_call_target="tpu_custom_call" | custom-call | tf_op jit(solution)/shard_map/finish/pallas_call | solution.py:382
  (6 shorter events, 0.1 us)
Async XLA Ops:
  0.6 0.8 %copy-start = (bf16[4,16,256]{2,1,0:T(8,128)(2,1)S(1)}, bf16[4,16,256]{2,1,0:T(8,128)(2,1)}, u32[]{:S(2)}) copy-start(bf16[4,16,256]{2,1,0:T(8,128)(2,1)} %param.6) | copy-start | bytes 98308
  1.4 0.7 %copy-start.1 = (bf16[2,8,256]{2,1,0:T(8,128)(2,1)S(1)}, bf16[2,8,256]{2,1,0:T(8,128)(2,1)}, u32[]{:S(2)}) copy-start(bf16[2,8,256]{2,1,0:T(8,128)(2,1)} %param.5) | copy-start | bytes 24580
  2.1 30.4 %copy-start.4 = (f32[8]{0:T(128)S(1)}, f32[8]{0:T(128)}, u32[]{:S(2)}) copy-start(f32[8]{0:T(128)} %param.8) | copy-start | bytes 100
  2.1 30.5 %copy-start.2 = (f32[8,3,3,3,3]{0,4,3,2,1:T(4,128)S(1)}, f32[8,3,3,3,3]{0,4,3,2,1:T(4,128)}, u32[]{:S(2)}) copy-start(f32[8,3,3,3,3]{0,4,3,2,1:T(4,128)} %param.7) | copy-start | bytes 7780
  2.1 30.5 %copy-start.3 = (f32[8,3,3,3,3]{0,4,3,2,1:T(4,128)S(1)}, f32[8,3,3,3,3]{0,4,3,2,1:T(4,128)}, u32[]{:S(2)}) copy-start(f32[8,3,3,3,3]{0,4,3,2,1:T(4,128)} %param.9) | copy-start | bytes 7780
  2.8 17.6 %all-to-all-start = ((bf16[8,80,256]{2,1,0:T(8,128)(2,1)}), bf16[8,80,256]{2,1,0:T(8,128)(2,1)S(1)}, u32[]{:S(2)}, u32[]{:S(2)}) async-start(bf16[8,80,256]{2,1,0:T(8,128)(2,1)} %spread.1), calls=%async_computation | async-start | bytes 655360 | tf_op jit(solution)/shard_map/all_to_all | solution.py:445
  20.5 8.7 %collective-permute-start.1 = (bf16[8,48,256]{2,1,0:T(8,128)(2,1)S(1)}, bf16[8,48,256]{2,1,0:T(8,128)(2,1)S(1)}, u32[]{:S(2)}, u32[]{:S(2)}) collective-permute-start(bf16[8,48,256]{2,1,0:T(8,128)(2,1)S(1)} %get-tuple-element.30), channel_id=1, source_target_pairs={{0,3},{1,2},{2,1},{3,0},{4,7},{5,6},{6,5},{7,4},{8,11},{9,10},{10,... | collective-permute-start | bytes 589832 | tf_op jit(solution)/shard_map/ppermute | solution.py:416
  20.6 8.6 %collective-permute-start = (bf16[8,48,256]{2,1,0:T(8,128)(2,1)S(1)}, bf16[8,48,256]{2,1,0:T(8,128)(2,1)S(1)}, u32[]{:S(2)}, u32[]{:S(2)}) collective-permute-start(bf16[8,48,256]{2,1,0:T(8,128)(2,1)S(1)} %get-tuple-element.31), channel_id=1, source_target_pairs={{0,1},{1,0},{2,3},{3,2},{4,5},{5,4},{6,7},{7,6},{8,9},{9,8},{10,11... | collective-permute-start | bytes 589832 | tf_op jit(solution)/shard_map/ppermute | solution.py:416
  22.2 7.0 %collective-permute-start.2 = (bf16[8,16,256]{2,1,0:T(8,128)(2,1)S(1)}, bf16[8,16,256]{2,1,0:T(8,128)(2,1)S(1)}, u32[]{:S(2)}, u32[]{:S(2)}) collective-permute-start(bf16[8,16,256]{2,1,0:T(8,128)(2,1)S(1)} %slice.12), channel_id=1, source_target_pairs={{0,2},{1,3},{2,0},{3,1},{4,6},{5,7},{6,4},{7,5},{8,10},{9,11},{10,... | collective-permute-start | bytes 196616 | tf_op jit(solution)/shard_map/ppermute | solution.py:416
  30.3 3.8 %collective-permute-start.5 = (f32[8,256]{1,0:T(8,128)S(1)}, f32[8,256]{1,0:T(8,128)S(1)}, u32[]{:S(2)}, u32[]{:S(2)}) collective-permute-start(f32[8,256]{1,0:T(8,128)S(1)} %get-tuple-element.16.refs_0_), channel_id=1, source_target_pairs={{0,2},{1,3},{2,0},{3,1},{4,6},{5,7},{6,4},{7,5},{8,10},{9,11},{10,... | collective-permute-start | bytes 24584 | tf_op jit(solution)/shard_map/ppermute | solution.py:416
  30.4 3.8 %collective-permute-start.4 = (f32[8,256]{1,0:T(8,128)S(1)}, f32[8,256]{1,0:T(8,128)S(1)}, u32[]{:S(2)}, u32[]{:S(2)}) collective-permute-start(f32[8,256]{1,0:T(8,128)S(1)} %get-tuple-element.16.refs_0_), channel_id=1, source_target_pairs={{0,3},{1,2},{2,1},{3,0},{4,7},{5,6},{6,5},{7,4},{8,11},{9,10},{10,... | collective-permute-start | bytes 24584 | tf_op jit(solution)/shard_map/ppermute | solution.py:416
  31.8 2.4 %collective-permute-start.3 = (f32[8,256]{1,0:T(8,128)S(1)}, f32[8,256]{1,0:T(8,128)S(1)}, u32[]{:S(2)}, u32[]{:S(2)}) collective-permute-start(f32[8,256]{1,0:T(8,128)S(1)} %get-tuple-element.16.refs_0_), channel_id=1, source_target_pairs={{0,1},{1,0},{2,3},{3,2},{4,5},{5,4},{6,7},{7,6},{8,9},{9,8},{10,11... | collective-permute-start | bytes 24584 | tf_op jit(solution)/shard_map/ppermute | solution.py:416
  38.7 10.3 %all-to-all-start.1 = ((f32[8,8,128]{2,1,0:T(8,128)}), f32[8,8,128]{2,1,0:T(8,128)S(1)}, u32[]{:S(2)}, u32[]{:S(2)}) async-start(f32[8,8,128]{2,1,0:T(8,128)} %get-tuple-element.23), calls=%async_computation.1 | async-start | bytes 65536 | tf_op jit(solution)/shard_map/all_to_all | solution.py:476
  42.6 1.9 %collective-permute-start.6 = (f32[48,256]{1,0:T(8,128)S(1)}, f32[48,256]{1,0:T(8,128)S(1)}, u32[]{:S(2)}, u32[]{:S(2)}) collective-permute-start(f32[48,256]{1,0:T(8,128)S(1)} %get-tuple-element.25), channel_id=1, source_target_pairs={{0,1},{1,0},{2,3},{3,2},{4,5},{5,4},{6,7},{7,6},{8,9},{9,8},{10,11... | collective-permute-start | bytes 147464 | tf_op jit(solution)/shard_map/ppermute | solution.py:416
  42.6 4.2 %collective-permute-start.7 = (f32[48,256]{1,0:T(8,128)S(1)}, f32[48,256]{1,0:T(8,128)S(1)}, u32[]{:S(2)}, u32[]{:S(2)}) collective-permute-start(f32[48,256]{1,0:T(8,128)S(1)} %get-tuple-element.26), channel_id=1, source_target_pairs={{0,2},{1,3},{2,0},{3,1},{4,6},{5,7},{6,4},{7,5},{8,10},{9,11},{10,... | collective-permute-start | bytes 147464 | tf_op jit(solution)/shard_map/ppermute | solution.py:416
  44.0 3.7 %collective-permute-start.8 = (f32[48,256]{1,0:T(8,128)S(1)}, f32[48,256]{1,0:T(8,128)S(1)}, u32[]{:S(2)}, u32[]{:S(2)}) collective-permute-start(f32[48,256]{1,0:T(8,128)S(1)} %get-tuple-element.27), channel_id=1, source_target_pairs={{0,3},{1,2},{2,1},{3,0},{4,7},{5,6},{6,5},{7,4},{8,11},{9,10},{10,... | collective-permute-start | bytes 147464 | tf_op jit(solution)/shard_map/ppermute | solution.py:416
